TPU v7x, 512 devices: a whole 4x8x8 slice. The times are simulated.
512 devices in a mesh: section: 4 (over x), frame: 8 (over z_hi, core), patch: 16 (over z_lo, y).
Axes of the slice: x: 4, y: 8, z: 8 (z_hi: 4, z_lo: 2; z = z_hi * 2 + z_lo), core: 2. Of those that a mesh axis runs over, the one named last changes fastest.
Arguments:
- exposure: bfloat16 [8, 2, 3584, 4096], P('frame', None, ('section', 'patch')), may hold values from -6 to 6, as said below
- row_prof: bfloat16 [8, 1280, 50, 64], P('frame', ('section', 'patch')), may hold values from -0.875 to 0.875
- col_prof: bfloat16 [8, 1280, 25, 256], P('frame', ('section', 'patch')), may hold values from -1.25 to 1.25
- row_off: int32 [8, 1280], P('frame', ('section', 'patch')), may hold values from 0 to 8, as said below
- col_off: int32 [8, 1280], P('frame', ('section', 'patch')), may hold values from 0 to 3840, as said below
- dest: int32 [8, 1280], P('frame', ('section', 'patch')), may hold values from 0 to 15, as said below
- fibre_weight: float32 [8, 1280, 25], P('frame', ('section', 'patch')), may hold values from 0.2 to 5
Outputs:
- spectra_ext: float32 [8, 2048, 50, 25], P('frame', ('section', 'patch'))
- coadd: float32 [1280, 50, 25], P(('section', 'patch'))
Inputs may be any that keep to these rules, and one draw needn't show every extreme that they name: `exposure`: channel 0 holds pixel values, channel 1 inverse variances between 0.25 and 4. `row_off`: offsets of patches within their band extended by 8 rows on each side. `col_off`: patches of neighbouring fibre blocks share columns. `dest`: of the 20 patches of one band (p // 20 equal) in one frame, each patch index receives 20 // 16 or (35) // 16 of them, so at most 2, and some index exactly 2.
All inputs are finite; a program needn't handle non-finite values.
Results may differ from a plain program's by a relative error of at most 0.0003.
Values may be sent and summed in bfloat16 or wider, within the bound.
A program may use at most 64 MiB of HBM per device.

v0:
```python
import jax
import jax.numpy as jnp
from jax import lax
from jax.sharding import PartitionSpec as P

HALO = 8
PC = 256
ITERS = 6
PR = 64


def padded(block, sides, width):
    for axis, dim in sides:
        count = lax.axis_size(axis)
        forward = [(i, i + 1) for i in range(count - 1)]
        backward = [(target, source) for source, target in forward]
        low = lax.ppermute(
            lax.slice_in_dim(block, block.shape[dim] - width, None, axis=dim), axis, forward
        )
        high = lax.ppermute(lax.slice_in_dim(block, 0, width, axis=dim), axis, backward)
        block = jnp.concatenate([low, block, high], axis=dim)
    return block


def solve_batch(pixels, row_psf, col_psf):
    highest = lax.Precision.HIGHEST
    values = pixels[..., 0, :, :].astype(jnp.float32)
    inverse = pixels[..., 1, :, :].astype(jnp.float32)
    row_float = row_psf.astype(jnp.float32)
    col_float = col_psf.astype(jnp.float32)
    folded = jnp.einsum("...wr,...rc->...wc", row_float, inverse * values, precision=highest)
    rhs_side = jnp.einsum("...wc,...fc->...wf", folded, col_float, precision=highest)
    estimate = jnp.zeros_like(rhs_side)
    residual = rhs_side
    direction = rhs_side
    norm_now = jnp.sum(residual * residual, axis=(-2, -1), keepdims=True)
    for sweep in range(ITERS):
        across = jnp.einsum("...wf,...fc->...wc", direction, col_float, precision=highest)
        modeled = jnp.einsum("...wr,...wc->...rc", row_float, across, precision=highest)
        normal_folded = jnp.einsum(
            "...wr,...rc->...wc", row_float, inverse * modeled, precision=highest
        )
        imaged = jnp.einsum("...wc,...fc->...wf", normal_folded, col_float, precision=highest)
        curvature = jnp.sum(direction * imaged, axis=(-2, -1), keepdims=True)
        step_size = norm_now / jnp.where(curvature > 0.0, curvature, 1.0)
        estimate = estimate + step_size * direction
        residual = residual - step_size * imaged
        norm_next = jnp.sum(residual * residual, axis=(-2, -1), keepdims=True)
        direction = residual + norm_next / jnp.where(norm_now > 0.0, norm_now, 1.0) * direction
        norm_now = norm_next
    return estimate


def cut_patch(frame_rows, first_row, first_col):
    zero_index = jnp.zeros((), jnp.int32)
    return lax.dynamic_slice(frame_rows, (zero_index, first_row, first_col), (2, PR, PC))


def pick_rows(table, rows):
    return table[rows]


def local(exposure, row_prof, col_prof, row_off, col_off, dest, fibre_weight):
    extended = padded(exposure, ((("section", "patch"), 2),), HALO)
    blocks = jax.vmap(jax.vmap(cut_patch, (None, 0, 0)), (0, 0, 0))(extended, row_off, col_off)
    group = lax.axis_size("patch")
    owned_count = dest.shape[1]
    capacity = (owned_count + group - 1) // group
    same = dest[:, :, None] == dest[:, None, :]
    patch_ids = jnp.arange(owned_count, dtype=jnp.int32)
    earlier = patch_ids[None, :] < patch_ids[:, None]
    slot_index = jnp.sum((same & earlier[None]).astype(jnp.int32), axis=-1)
    dest_ids = jnp.arange(group, dtype=jnp.int32)
    slot_ids = jnp.arange(capacity, dtype=jnp.int32)
    chosen = (dest[:, None, None, :] == dest_ids[None, :, None, None]) & (
        slot_index[:, None, None, :] == slot_ids[None, None, :, None]
    )
    source = jnp.sum(jnp.where(chosen, patch_ids[None, None, None, :], 0), axis=-1)
    filled = jnp.any(chosen, axis=-1)
    owned = solve_batch(blocks, row_prof, col_prof)
    picked = jax.vmap(pick_rows)(owned, source)
    weight_mask = filled.reshape(filled.shape + (1,) * (picked.ndim - 3)).astype(picked.dtype)
    received = lax.all_to_all(
        picked * weight_mask, "patch", split_axis=1, concat_axis=1, tiled=True
    )
    spectra_ext = received.reshape(
        received.shape[0], group * capacity, received.shape[3], received.shape[4]
    )
    numerator = jnp.sum(fibre_weight[:, :, None, :] * owned, axis=0)
    denominator = jnp.sum(fibre_weight, axis=0)
    totals = lax.psum((numerator, denominator), "frame")
    coadd = totals[0] / totals[1][:, None, :]
    return (spectra_ext, coadd)


def solution(mesh):
    in_specs = (
        P("frame", None, ("section", "patch"), None),
        P("frame", ("section", "patch"), None, None),
        P("frame", ("section", "patch"), None, None),
        P("frame", ("section", "patch")),
        P("frame", ("section", "patch")),
        P("frame", ("section", "patch")),
        P("frame", ("section", "patch"), None),
    )
    out_specs = (P("frame", ("section", "patch"), None, None), P(("section", "patch"), None, None))
    return jax.shard_map(local, mesh=mesh, in_specs=in_specs, out_specs=out_specs, check_vma=False)
```

profile of v0, /device:TPU:1, one launch (start us, length us, event | category | flops | bytes accessed | tf_op | source)
XLA Modules:
  0.0 183.3 jit_solution(1677671176419128398)
XLA Ops:
  7.2 1.0 fusion.66
  8.3 4.0 %collective-permute-start = (bf16[1,2,8,4096]{3,2,1,0:T(8,128)(2,1)S(1)}, bf16[1,2,8,4096]{3,2,1,0:T(8,128)(2,1)S(1)}, u32[]{:S(2)}, u32[]{:S(2)}) collective-permute-start(bf16[1,2,8,4096]{3,2,1,0:T(8,128)(2,1)S(1)} %get-tuple-element.42), channel_id=1, source_target_pairs={{0,1},{1,2},{2,3},{3,4},{4,5},{5,6},{6,7},{7,8},{8,9},{9,10},{10,1... | collective-permute-start | bytes 393224 | tf_op jit(solution)/shard_map/ppermute | solution.py:17
  12.3 1.3 collective-permute-start.1
  13.6 0.7 iota_compare_fusion
  14.3 1.2 fusion.23
  15.7 0.7 fusion.27
  16.5 0.7 copy.157
  18.0 1.3 pad_maximum_fusion
  19.3 42.7 %while.1 = (s32[]{:T(128)}, bf16[1,2,72,4096]{3,2,1,0:T(8,128)(2,1)S(1)}, s32[20,4]{0,1:T(4,128)S(1)}, bf16[20,2,64,256]{3,2,0,1:T(8,128)(2,1)S(1)}, s32[]{:T(128)}) while((s32[]{:T(128)}, bf16[1,2,72,4096]{3,2,1,0:T(8,128)(2,1)S(1)}, s32[20,4]{0,1:T(4,128)S(1)}, bf16[20,2,64,256]{3,2,0,1:T(8,128)(2,1)S(1)}, s32[]{:T(128)}) %tuple.41), condition=%wide.while_cond, body=%wide.while_body.sunk | while | flops 2 | bytes 131197 | solution.py:56
  20.0 1.4 bitcast_dynamic-update-slice_fusion.2
  22.1 1.4 bitcast_dynamic-update-slice_fusion.2
  24.2 1.4 bitcast_dynamic-update-slice_fusion.2
  26.4 1.4 bitcast_dynamic-update-slice_fusion.2
  28.5 1.4 bitcast_dynamic-update-slice_fusion.2
  30.6 1.4 bitcast_dynamic-update-slice_fusion.2
  32.8 1.4 bitcast_dynamic-update-slice_fusion.2
  34.9 1.4 bitcast_dynamic-update-slice_fusion.2
  37.1 1.4 bitcast_dynamic-update-slice_fusion.2
  39.2 1.4 bitcast_dynamic-update-slice_fusion.2
  41.3 1.4 bitcast_dynamic-update-slice_fusion.2
  43.5 1.4 bitcast_dynamic-update-slice_fusion.2
  45.6 1.4 bitcast_dynamic-update-slice_fusion.2
  47.7 1.4 bitcast_dynamic-update-slice_fusion.2
  49.9 1.4 bitcast_dynamic-update-slice_fusion.2
  52.0 1.4 bitcast_dynamic-update-slice_fusion.2
  54.1 1.4 bitcast_dynamic-update-slice_fusion.2
  56.3 1.4 bitcast_dynamic-update-slice_fusion.2
  58.4 1.4 bitcast_dynamic-update-slice_fusion.2
  60.5 1.4 bitcast_dynamic-update-slice_fusion.2
  62.0 0.8 fusion
  62.9 0.7 fusion.63
  63.6 0.7 fusion.61
  64.3 0.9 convert_multiply_fusion.5
  65.1 0.7 fusion.18
  65.9 0.9 multiply_reduce_fusion.9
  67.3 0.7 fusion.57
  67.9 0.9 convert_multiply_fusion.4
  68.8 0.7 fusion.15
  69.5 0.9 multiply_reduce_fusion.7
  70.9 0.7 fusion.53
  71.6 0.9 convert_multiply_fusion.3
  72.4 0.7 fusion.12
  73.1 0.9 multiply_reduce_fusion.5
  74.5 0.7 fusion.49
  75.1 1.1 convert_multiply_fusion.2
  76.2 0.7 fusion.9
  76.9 0.9 multiply_reduce_fusion.3
  78.2 0.7 fusion.45
  78.9 0.9 convert_multiply_fusion.1
  79.8 0.7 fusion.6
  80.5 0.9 multiply_reduce_fusion.1
  81.9 0.7 fusion.41
  82.5 0.9 convert_multiply_fusion
  83.4 0.7 fusion.3
  84.1 0.9 fusion.2
  85.0 1.0 broadcast_multiply_fusion
  87.0 1.3 reshape.637
  88.4 10.3 %all-to-all-start = ((f32[16,1,2500]{2,1,0:T(1,128)}), f32[16,1,2500]{2,1,0:T(1,128)S(1)}, u32[]{:S(2)}, u32[]{:S(2)}) async-start(f32[16,1,2500]{2,1,0:T(1,128)} %reshape.637), calls=%async_computation | async-start | bytes 327680 | tf_op jit(solution)/shard_map/all_to_all | solution.py:83
  98.7 31.2 %psum.15 = f32[20,25]{1,0:T(8,128)S(1)} all-reduce(f32[20,25]{1,0:T(8,128)S(1)} %bitcast.162), channel_id=1, replica_groups=mesh['section'=4,'frame'=8,'patch'=16] {'frame'}, use_global_device_ids=true, to_apply=%region_16.17 | all-reduce | flops 500 | bytes 4000 | tf_op jit(solution)/shard_map/psum | solution.py:91
  129.9 41.7 %all-reduce.2.cloned.1.call-done = f32[20,50,25]{1,2,0:T(8,128)} async-done(((f32[20,50,25]{1,2,0:T(8,128)}), f32[20,50,25]{1,2,0:T(8,128)}) %all-reduce.2.cloned.1.call-update) | async-done | bytes 100016 | tf_op jit(solution)/shard_map/psum | solution.py:91
  171.6 1.1 broadcast_divide_fusion
  172.7 0.9 copy.111
  174.1 1.0 reduce.27
  175.5 1.0 copy.110
  (88 shorter events, 18.8 us)
Async XLA Ops:
  7.2 55.7 %copy-start = (bf16[1,20,25,256]{3,1,2,0:T(8,128)(2,1)S(1)}, bf16[1,20,25,256]{3,1,2,0:T(8,128)(2,1)}, u32[]{:S(2)}) copy-start(bf16[1,20,25,256]{3,1,2,0:T(8,128)(2,1)} %param.9) | copy-start | bytes 768004
  7.2 164.4 %all-reduce.2.cloned.1.call-start = ((), (), s32[]{:S(2)}) async-start(), calls=%async_computation.1 | async-start | bytes 655360 | tf_op jit(solution)/shard_map/psum | solution.py:91
  8.3 9.3 %collective-permute-start = (bf16[1,2,8,4096]{3,2,1,0:T(8,128)(2,1)S(1)}, bf16[1,2,8,4096]{3,2,1,0:T(8,128)(2,1)S(1)}, u32[]{:S(2)}, u32[]{:S(2)}) collective-permute-start(bf16[1,2,8,4096]{3,2,1,0:T(8,128)(2,1)S(1)} %get-tuple-element.42), channel_id=1, source_target_pairs={{0,1},{1,2},{2,3},{3,4},{4,5},{5,6},{6,7},{7,8},{8,9},{9,10},{10,1... | collective-permute-start | bytes 393224 | tf_op jit(solution)/shard_map/ppermute | solution.py:17
  12.3 5.7 %collective-permute-start.1 = (bf16[1,2,8,4096]{3,2,1,0:T(8,128)(2,1)S(1)}, bf16[1,2,8,4096]{3,2,1,0:T(8,128)(2,1)S(1)}, u32[]{:S(2)}, u32[]{:S(2)}) collective-permute-start(bf16[1,2,8,4096]{3,2,1,0:T(8,128)(2,1)S(1)} %get-tuple-element.43), channel_id=1, source_target_pairs={{1,0},{2,1},{3,2},{4,3},{5,4},{6,5},{7,6},{8,7},{9,8},{10,9},{11,1... | collective-permute-start | bytes 393224 | tf_op jit(solution)/shard_map/ppermute | solution.py:20
  17.5 44.5 %copy-start.1 = (bf16[1,20,50,64]{3,2,1,0:T(8,128)(2,1)S(1)}, bf16[1,20,50,64]{3,2,1,0:T(8,128)(2,1)}, u32[]{:S(2)}) copy-start(bf16[1,20,50,64]{3,2,1,0:T(8,128)(2,1)} %param.8) | copy-start | bytes 384004
  88.4 85.2 %all-to-all-start = ((f32[16,1,2500]{2,1,0:T(1,128)}), f32[16,1,2500]{2,1,0:T(1,128)S(1)}, u32[]{:S(2)}, u32[]{:S(2)}) async-start(f32[16,1,2500]{2,1,0:T(1,128)} %reshape.637), calls=%async_computation | async-start | bytes 327680 | tf_op jit(solution)/shard_map/all_to_all | solution.py:83
Sparse Core Ops, SparseCore 0:
  86.2 85.3 all-reduce.1
where the time goes:
time: 184 us; the launch traced here: 183 us
  local copies, waits for them, and re-layouts  49 us (27%)
  waiting for transfers between devices  42.1 us (23%)
  blocking collectives  31.2 us (17%)
  matrix products  20.4 us (11%)
  starting transfers between devices  15.7 us (9%)
  between operations  14.4 us (8%)
  other arithmetic  10.1 us (5%)
    gather x60, local copies, waits for them, and re-layouts  42.3 us
    psum x1, waiting for transfers between devices, local(): totals = lax.psum((numerator, denominator), 'frame')  41.7 us
    psum x1, blocking collectives, local(): totals = lax.psum((numerator, denominator), 'frame')  31.2 us
    all_to_all x1, starting transfers between devices, local(): lax.all_to_all(picked * weight_mask, 'patch', split_axis=1, concat_axis=1...  10.3 us
    dot_general x6, matrix products, solve_batch(): jnp.einsum('...wr,...wc->...rc', row_float, across, precision=highest)  5.32 us
    dot_general x6, matrix products, solve_batch(): jnp.einsum('...wc,...fc->...wf', normal_folded, col_float, precision=high...  5.18 us
    dot_general x6, matrix products, solve_batch(): jnp.einsum('...wr,...rc->...wc', row_float, inverse * modeled, precision=...  4.34 us
    ppermute x1, starting transfers between devices, padded(): lax.ppermute(lax.slice_in_dim(block, block.shape[dim] - width, None, axis...  4.03 us
  transfers between devices with their start and end apart: 4, of which 2 were waited for; matrix products, arithmetic and copies ran while one was open for 4% of the time, Pallas kernels for 0%

commit v1 on v0

v1 whole, which is shorter than its diff:
```python
import functools

import jax
import jax.numpy as jnp
from jax import lax
from jax.experimental import pallas as pl
from jax.experimental.pallas import tpu as pltpu
from jax.sharding import PartitionSpec as P

HALO = 8
PC = 256
ITERS = 6
PR = 64
LANES = 128
WPB = 50
FPB = 25
MESH = pl.DeviceIdType.MESH
NT = (((1,), (1,)), ((), ()))


def halo_rows(block, width):
    axes = ("section", "patch")
    count = lax.axis_size(axes)
    forward = [(i, i + 1) for i in range(count - 1)]
    backward = [(target, source) for source, target in forward]
    rows = block.shape[2]
    low = lax.ppermute(lax.slice_in_dim(block, rows - width, None, axis=2), axes, forward)
    high = lax.ppermute(lax.slice_in_dim(block, 0, width, axis=2), axes, backward)
    return low[0], high[0]


def lane_index(shape):
    return lax.broadcasted_iota(jnp.int32, shape, len(shape) - 1)


def second_piece(value, first):
    head = value.astype(jnp.bfloat16).astype(jnp.float32)
    return jnp.where(first, value, value - head).astype(jnp.bfloat16)


def project(weighted, cols, profile, half):
    head = weighted.astype(jnp.bfloat16)
    tail = (weighted - head.astype(jnp.float32)).astype(jnp.bfloat16)
    both = jnp.concatenate([head, tail], axis=0)
    folded = lax.dot_general(cols, both, NT, preferred_element_type=jnp.float32)
    folded = folded + pltpu.roll(folded, LANES // 2, 1)
    return jnp.dot(
        second_piece(folded, half),
        jnp.concatenate([profile, profile], axis=0),
        preferred_element_type=jnp.float32,
    )


def image_of(direction, cols, profile, half, quarter):
    pieces = second_piece(direction, half)
    pieces = jnp.concatenate([pieces, pieces], axis=0)
    across = lax.dot_general(profile, pieces, NT, preferred_element_type=jnp.float32)
    return jnp.dot(
        second_piece(across, quarter),
        jnp.concatenate([cols, cols], axis=0),
        preferred_element_type=jnp.float32,
    )


def total(value):
    return jnp.sum(jnp.sum(value, axis=0, keepdims=True), axis=1, keepdims=True)


def solve_kernel(
    count, group, row_off, col_off, dest, expo, low, high, profile, cols, weight,
    send, contrib,
    ext, inverse, direction, residual, spectra, norms, source, filled,
):
    half = lane_index((32, LANES)) < LANES // 2
    quarter = lane_index((PR, PR)) < PR // 2
    lanes = lane_index((PR, LANES))
    tiles = expo.shape[2] // LANES
    for channel in range(2):
        for tile in range(tiles):
            at = slice(tile * LANES, (tile + 1) * LANES)
            ext[channel, tile, 0:HALO, :] = low[channel, :, at].astype(jnp.float32)
            ext[channel, tile, HALO:PR, :] = expo[channel, :, at].astype(jnp.float32)
            ext[channel, tile, PR:PR + HALO, :] = high[channel, :, at].astype(jnp.float32)

    for d in range(group):
        filled[d] = 0
        source[2 * d] = count
        source[2 * d + 1] = count
    for p in range(count):
        target = dest[p]
        slot = filled[target]
        source[2 * target + slot] = p
        filled[target] = slot + 1

    def cut(channel, first_tile, row, shift):
        moved = [
            pltpu.roll(ext[channel, first_tile + j, pl.ds(row, PR), :], LANES - shift, 1)
            for j in range(3)
        ]
        keep = lanes < LANES - shift
        return jnp.concatenate(
            [jnp.where(keep, moved[0], moved[1]), jnp.where(keep, moved[1], moved[2])], axis=1
        )

    for p in range(count):
        row, col = row_off[p], col_off[p]
        first_tile = col // LANES
        shift = col - first_tile * LANES
        weights = cut(1, first_tile, row, shift)
        inverse[p] = weights
        rhs = project(weights * cut(0, first_tile, row, shift), cols[p], profile[p], half)
        direction[p] = rhs
        residual[p] = rhs
        spectra[p] = jnp.zeros_like(rhs)
        norms[p] = jnp.broadcast_to(total(rhs * rhs), (8, LANES))
    spectra[count] = jnp.zeros((32, LANES), jnp.float32)

    def sweep(step, carry):
        for p in range(count):
            along = direction[p]
            modeled = image_of(along, cols[p], profile[p], half, quarter)
            imaged = project(inverse[p] * modeled, cols[p], profile[p], half)
            curvature = total(along * imaged)
            now = norms[p][0:1, 0:1]
            size = now / jnp.where(curvature > 0.0, curvature, 1.0)
            spectra[p] += size * along
            left = residual[p] - size * imaged
            residual[p] = left
            later = total(left * left)
            norms[p] = jnp.broadcast_to(later, (8, LANES))
            direction[p] = left + later / jnp.where(now > 0.0, now, 1.0) * along
        return carry

    lax.fori_loop(0, ITERS - 1, sweep, 0)
    for p in range(count):
        along = direction[p]
        modeled = image_of(along, cols[p], profile[p], half, quarter)
        curvature = 2.0 * total(jnp.sum(inverse[p] * modeled * modeled, axis=0, keepdims=True))
        spectra[p] += norms[p][0:1, 0:1] / jnp.where(curvature > 0.0, curvature, 1.0) * along

    for d in range(group):
        first = spectra[source[2 * d]]
        other = spectra[source[2 * d + 1]]
        send[d] = jnp.where(half, first, other)[0:FPB]

    pairs = count // 2
    per_half = pairs // 2
    marked = lane_index((32, LANES)) % (LANES // 2) == WPB
    for j in range(pairs):
        first = jnp.broadcast_to(weight[:, j:j + 1], (32, LANES))
        other = jnp.broadcast_to(weight[:, pairs + j:pairs + j + 1], (32, LANES))
        scale = jnp.where(half, first, other)
        value = scale * jnp.where(marked, 1.0, jnp.where(half, spectra[j], spectra[pairs + j]))
        start = (j % per_half) * FPB
        contrib[j // per_half, start:start + FPB, :] = value[0:FPB]
    for h in range(2):
        contrib[h, per_half * FPB:, :] = jnp.zeros((LANES - per_half * FPB, LANES), jnp.float32)


def exchange_kernel(group, frames, send, contrib, recv, sums, arrived, gathered, out_sem, in_sem,
                    pair_sem, peer_out, peer_in, back_sem):
    me = lax.axis_index("patch")
    frame = lax.axis_index("frame")
    core = lax.rem(frame, 2)
    chip = frame // 2
    chips = frames // 2
    partner = frame + 1 - 2 * core
    barrier = pltpu.get_barrier_semaphore()
    for k in range(1, group):
        pl.semaphore_signal(barrier, inc=1, device_id={"patch": lax.rem(me + k, group)}, device_id_type=MESH)
    pl.semaphore_signal(barrier, inc=1, device_id={"frame": partner}, device_id_type=MESH)
    for k in range(1, chips):
        pl.semaphore_signal(barrier, inc=1, device_id={"frame": lax.rem(frame + 2 * k, frames)}, device_id_type=MESH)
    pl.semaphore_wait(barrier, group + chips - 1)

    swap = pltpu.make_async_remote_copy(
        contrib.at[1 - core], arrived, pair_sem.at[0], pair_sem.at[1],
        device_id={"frame": partner}, device_id_type=MESH)
    swap.start()
    copies = []
    for k in range(1, group):
        to = lax.rem(me + k, group)
        copies.append(pltpu.make_async_remote_copy(
            send.at[to], recv.at[me], out_sem.at[k], in_sem.at[k],
            device_id={"patch": to}, device_id_type=MESH))
        copies[-1].start()
    recv[me] = send[me]
    swap.wait()
    gathered[chip] = contrib[core] + arrived[...]
    peers = []
    for k in range(1, chips):
        peers.append(pltpu.make_async_remote_copy(
            gathered.at[chip], gathered.at[chip], peer_out.at[k], peer_in.at[k],
            device_id={"frame": lax.rem(frame + 2 * k, frames)}, device_id_type=MESH))
        peers[-1].start()
    for copy in peers:
        copy.wait()
    whole = gathered[0]
    for k in range(1, chips):
        whole = whole + gathered[k]
    sums[core] = whole
    back = pltpu.make_async_remote_copy(
        sums.at[core], sums.at[core], back_sem.at[0], back_sem.at[1],
        device_id={"frame": partner}, device_id_type=MESH)
    back.start()
    for copy in copies:
        copy.wait()
    back.wait()


def format_kernel(count, group, recv, sums, ext_out, coadd_out):
    pairs = count // 2
    per_half = pairs // 2
    for k in range(FPB):
        rows = recv[:, k, :]
        ext_out[k, pl.ds(0, group, stride=2), :] = rows[:, 0:WPB]
        ext_out[k, pl.ds(1, group, stride=2), :] = pltpu.roll(rows, LANES // 2, 1)[:, 0:WPB]
        for h in range(2):
            rows = sums[h, pl.ds(k, per_half, stride=FPB), :]
            for s in range(2):
                here = rows if s == 0 else pltpu.roll(rows, LANES // 2, 1)
                start = s * pairs + h * per_half
                coadd_out[k, start:start + per_half, :] = here[:, 0:WPB] / here[:, WPB:WPB + 1]


VMEM = pl.BlockSpec(memory_space=pltpu.VMEM)
SMEM = pl.BlockSpec(memory_space=pltpu.SMEM)


def local(exposure, row_prof, col_prof, row_off, col_off, dest, fibre_weight):
    group = lax.axis_size("patch")
    frames = lax.axis_size("frame")
    count = dest.shape[1]
    f32 = jnp.float32
    low, high = halo_rows(exposure, HALO)
    profile = jnp.swapaxes(row_prof[0], 1, 2)
    profile = jnp.pad(profile, ((0, 0), (0, 0), (0, LANES // 2 - WPB)))
    profile = jnp.concatenate([profile, profile], axis=2)
    cols = jnp.pad(col_prof[0], ((0, 0), (0, 32 - FPB), (0, 0)))
    weight = jnp.pad(fibre_weight[0].T, ((0, 32 - FPB), (0, LANES - count)))
    tiles = exposure.shape[3] // LANES
    send, contrib = pl.pallas_call(
        functools.partial(solve_kernel, count, group),
        out_shape=(
            jax.ShapeDtypeStruct((group, FPB, LANES), f32),
            jax.ShapeDtypeStruct((2, LANES, LANES), f32),
        ),
        in_specs=[SMEM] * 3 + [VMEM] * 6,
        out_specs=(VMEM, VMEM),
        scratch_shapes=[
            pltpu.VMEM((2, tiles + 1, PR + HALO, LANES), f32),
            pltpu.VMEM((count, PR, PC), f32),
            pltpu.VMEM((count, 32, LANES), f32),
            pltpu.VMEM((count, 32, LANES), f32),
            pltpu.VMEM((count + 1, 32, LANES), f32),
            pltpu.VMEM((count, 8, LANES), f32),
            pltpu.SMEM((2 * group,), jnp.int32),
            pltpu.SMEM((group,), jnp.int32),
        ],
        compiler_params=pltpu.CompilerParams(vmem_limit_bytes=40 << 20),
        name="solve",
    )(row_off[0], col_off[0], dest[0], exposure[0], low, high, profile, cols, weight)
    chips = frames // 2
    recv, sums = pl.pallas_call(
        functools.partial(exchange_kernel, group, frames),
        out_shape=(
            jax.ShapeDtypeStruct((group, FPB, LANES), f32),
            jax.ShapeDtypeStruct((2, LANES, LANES), f32),
        ),
        in_specs=[VMEM] * 2,
        out_specs=(VMEM, VMEM),
        scratch_shapes=[
            pltpu.VMEM((LANES, LANES), f32),
            pltpu.VMEM((chips, LANES, LANES), f32),
            pltpu.SemaphoreType.DMA((group,)),
            pltpu.SemaphoreType.DMA((group,)),
            pltpu.SemaphoreType.DMA((2,)),
            pltpu.SemaphoreType.DMA((chips,)),
            pltpu.SemaphoreType.DMA((chips,)),
            pltpu.SemaphoreType.DMA((2,)),
        ],
        compiler_params=pltpu.CompilerParams(collective_id=0, has_side_effects=True),
        name="exchange",
    )(send, contrib)
    ext_out, coadd_out = pl.pallas_call(
        functools.partial(format_kernel, count, group),
        out_shape=(
            jax.ShapeDtypeStruct((FPB, 2 * group, WPB), f32),
            jax.ShapeDtypeStruct((FPB, count, WPB), f32),
        ),
        in_specs=[VMEM] * 2,
        out_specs=(VMEM, VMEM),
        name="arrange",
    )(recv, sums)
    return jnp.transpose(ext_out, (1, 2, 0))[None], jnp.transpose(coadd_out, (1, 2, 0))


def solution(mesh):
    in_specs = (
        P("frame", None, ("section", "patch"), None),
        P("frame", ("section", "patch"), None, None),
        P("frame", ("section", "patch"), None, None),
        P("frame", ("section", "patch")),
        P("frame", ("section", "patch")),
        P("frame", ("section", "patch")),
        P("frame", ("section", "patch"), None),
    )
    out_specs = (P("frame", ("section", "patch"), None, None), P(("section", "patch"), None, None))
    return jax.shard_map(local, mesh=mesh, in_specs=in_specs, out_specs=out_specs, check_vma=False)
```

time: 184 us -> 110 us (0.60)
  Pallas kernels: 0 us -> 97.2 us
  local copies, waits for them, and re-layouts: 49 us -> 4.38 us
  waiting for transfers between devices: 42.1 us -> 0.43 us
  blocking collectives: 31.2 us -> 0 us
  matrix products: 20.4 us -> 0 us
  between operations: 14.4 us -> 0.76 us
  other arithmetic: 10.1 us -> 0.18 us
  starting transfers between devices: 15.7 us -> 5.95 us
    pallas_call x0 -> x3, Pallas kernels: none -> 97.2 us  [the longest x1 61.5 us: local(): pl.pallas_call(functools.partial(solve_kernel, count, group), out_shape=(...]
    gather x65 -> x0, local copies, waits for them, and re-layouts: 43.1 us -> none
    psum x1 -> x0, waiting for transfers between devices: 41.7 us -> none  [local(): totals = lax.psum((numerator, denominator), 'frame')]
    psum x1 -> x0, blocking collectives: 31.2 us -> none  [local(): totals = lax.psum((numerator, denominator), 'frame')]
    dot_general x26 -> x0, matrix products: 20.4 us -> none  [the longest x6 5.32 us: solve_batch(): jnp.einsum('...wr,...wc->...rc', row_float, across, precision=highest)]
    all_to_all x1 -> x0, starting transfers between devices: 10.3 us -> none  [local(): lax.all_to_all(picked * weight_mask, 'patch', split_axis=1, concat_axis=1...]
    reduce_sum x7 -> x0, other arithmetic: 3.03 us -> none  [the longest x5 1.67 us: solve_batch(): norm_next = jnp.sum(residual * residual, axis=(-2, -1), keepdims=True)]
  transfers between devices with their start and end apart: 4 -> 2, of which waited for: 2 -> 1; matrix products, arithmetic and copies ran while one was open for 4% -> 1% of each run, Pallas kernels for 0% -> 0%
where the time goes in v1:
time: 110 us; the launch traced here: 109 us
  Pallas kernels  97.2 us (88%)
  starting transfers between devices  5.95 us (5%)
  local copies, waits for them, and re-layouts  4.38 us (4%)
    pallas_call x1, Pallas kernels, local(): pl.pallas_call(functools.partial(solve_kernel, count, group), out_shape=(...  61.5 us
    pallas_call x1, Pallas kernels, local(): pl.pallas_call(functools.partial(exchange_kernel, group, frames), out_sha...  32 us
    ppermute x1, starting transfers between devices, halo_rows(): lax.ppermute(lax.slice_in_dim(block, rows - width, None, axis=2), axes, f...  4.65 us
    pallas_call x1, Pallas kernels, local(): pl.pallas_call(functools.partial(format_kernel, count, group), out_shape=...  3.61 us
    unnamed x21, local copies, waits for them, and re-layouts  3.24 us
  transfers between devices with their start and end apart: 2, of which 1 were waited for; matrix products, arithmetic and copies ran while one was open for 1% of the time, Pallas kernels for 0%

profile of v1, /device:TPU:1, one launch (start us, length us, event | category | flops | bytes accessed | tf_op | source)
XLA Modules:
  0.0 108.9 jit_solution(17719939103592873424)
XLA Ops:
  0.6 0.0 copy-start.7
  0.6 0.0 copy-start.8
  0.6 1.0 fusion
  1.7 1.3 %collective-permute-start.1 = (bf16[1,2,8,4096]{3,2,1,0:T(8,128)(2,1)S(1)}, bf16[1,2,8,4096]{3,2,1,0:T(8,128)(2,1)S(1)}, u32[]{:S(2)}, u32[]{:S(2)}) collective-permute-start(bf16[1,2,8,4096]{3,2,1,0:T(8,128)(2,1)S(1)} %get-tuple-element.14), channel_id=1, source_target_pairs={{1,0},{2,1},{3,2},{4,3},{5,4},{6,5},{7,6},{8,7},{9,8},{10,9},{11,1... | collective-permute-start | bytes 393224 | tf_op jit(solution)/shard_map/ppermute | solution.py:28
  3.0 4.7 %collective-permute-start = (bf16[1,2,8,4096]{3,2,1,0:T(8,128)(2,1)S(1)}, bf16[1,2,8,4096]{3,2,1,0:T(8,128)(2,1)S(1)}, u32[]{:S(2)}, u32[]{:S(2)}) collective-permute-start(bf16[1,2,8,4096]{3,2,1,0:T(8,128)(2,1)S(1)} %get-tuple-element.15), channel_id=1, source_target_pairs={{0,1},{1,2},{2,3},{3,4},{4,5},{5,6},{6,7},{7,8},{8,9},{9,10},{10,1... | collective-permute-start | bytes 393224 | tf_op jit(solution)/shard_map/ppermute | solution.py:27
  7.6 0.0 copy-done.8
  7.7 0.1 copy.11
  7.8 0.0 copy-done.7
  7.8 0.0 copy-start.6
  7.8 0.2 copy.9
  8.0 0.7 copy-done.6
  8.7 0.1 copy.13
  8.8 0.0 copy-start
  8.8 0.1 pad.12
  8.9 0.2 pad_maximum_fusion.profile
  9.1 0.0 collective-permute-done.1
  9.1 0.4 collective-permute-done
  9.6 0.0 copy-start.3
  9.6 0.0 copy-start.4
  9.6 0.0 copy-start.5
  9.6 0.4 copy-done
  10.0 0.3 copy-done.3
  10.3 0.0 copy-done.4
  10.3 0.0 copy-done.5
  10.3 61.5 %solve.1 = (f32[16,25,128]{2,1,0:T(8,128)S(1)}, f32[2,128,128]{2,1,0:T(8,128)S(1)}) custom-call(s32[20]{0:T(128)S(1)} %bitcast.22, s32[20]{0:T(128)S(1)} %bitcast.23, s32[20]{0:T(128)S(1)} %bitcast.24, bf16[2,56,4096]{2,1,0:T(8,128)(2,1)S(1)} %bitcast.19, bf16[2,8,4096]{2,1,0:T(8,128)(2,1)S(1)} %bitcast.21, bf16[2,8,4096]{2,1,0:T(8,128)(2,1)S(1)} %bitcast.20, ...), custom_call_target="tpu_custom_call" | custom-call | tf_op jit(solution)/shard_map/solve/pallas_call | solution.py:242
  71.9 0.0 copy-start.1
  71.9 0.7 copy-done.1
  72.6 0.0 copy-start.2
  72.6 0.7 copy-done.2
  73.2 32.0 %exchange.1 = (f32[16,25,128]{2,1,0:T(8,128)}, f32[2,128,128]{2,1,0:T(8,128)}) custom-call(f32[16,25,128]{2,1,0:T(8,128)} %copy-done.1, f32[2,128,128]{2,1,0:T(8,128)} %copy-done.2), custom_call_target="tpu_custom_call" | custom-call | tf_op jit(solution)/shard_map/exchange/pallas_call | solution.py:264
  105.3 3.6 %arrange.1 = (f32[25,32,50]{2,1,0:T(8,128)}, f32[25,20,50]{2,1,0:T(8,128)}) custom-call(f32[16,25,128]{2,1,0:T(8,128)} %get-tuple-element.10.recv, f32[2,128,128]{2,1,0:T(8,128)} %get-tuple-element.11.sums), custom_call_target="tpu_custom_call" | custom-call | tf_op jit(solution)/shard_map/arrange/pallas_call | solution.py:285
  (2 shorter events, 0.0 us)
Async XLA Ops:
  0.6 7.1 %copy-start.7 = (bf16[1,20,50,64]{3,2,1,0:T(8,128)(2,1)S(1)}, bf16[1,20,50,64]{3,2,1,0:T(8,128)(2,1)}, u32[]{:S(2)}) copy-start(bf16[1,20,50,64]{3,2,1,0:T(8,128)(2,1)} %param.8) | copy-start | bytes 384004
  0.6 7.0 %copy-start.8 = (f32[1,20,25]{2,0,1:T(1,128)S(1)}, f32[1,20,25]{2,0,1:T(1,128)}, u32[]{:S(2)}) copy-start(f32[1,20,25]{2,0,1:T(1,128)} %param.13) | copy-start | bytes 6004
  1.7 7.4 %collective-permute-start.1 = (bf16[1,2,8,4096]{3,2,1,0:T(8,128)(2,1)S(1)}, bf16[1,2,8,4096]{3,2,1,0:T(8,128)(2,1)S(1)}, u32[]{:S(2)}, u32[]{:S(2)}) collective-permute-start(bf16[1,2,8,4096]{3,2,1,0:T(8,128)(2,1)S(1)} %get-tuple-element.14), channel_id=1, source_target_pairs={{1,0},{2,1},{3,2},{4,3},{5,4},{6,5},{7,6},{8,7},{9,8},{10,9},{11,1... | collective-permute-start | bytes 393224 | tf_op jit(solution)/shard_map/ppermute | solution.py:28
  3.0 6.6 %collective-permute-start = (bf16[1,2,8,4096]{3,2,1,0:T(8,128)(2,1)S(1)}, bf16[1,2,8,4096]{3,2,1,0:T(8,128)(2,1)S(1)}, u32[]{:S(2)}, u32[]{:S(2)}) collective-permute-start(bf16[1,2,8,4096]{3,2,1,0:T(8,128)(2,1)S(1)} %get-tuple-element.15), channel_id=1, source_target_pairs={{0,1},{1,2},{2,3},{3,4},{4,5},{5,6},{6,7},{7,8},{8,9},{9,10},{10,1... | collective-permute-start | bytes 393224 | tf_op jit(solution)/shard_map/ppermute | solution.py:27
  7.8 1.0 copy-start.6
  8.8 1.2 %copy-start = (bf16[1,2,56,4096]{3,2,1,0:T(8,128)(2,1)S(1)}, bf16[1,2,56,4096]{3,2,1,0:T(8,128)(2,1)}, u32[]{:S(2)}) copy-start(bf16[1,2,56,4096]{3,2,1,0:T(8,128)(2,1)} %param.7) | copy-start | bytes 2752516
  9.6 0.7 copy-start.3
  9.6 0.7 copy-start.4
  9.6 0.8 copy-start.5
  71.9 0.7 copy-start.1
  72.6 0.7 copy-start.2

commit v2 on v1

--- a/solution.py
+++ b/solution.py
@@ -14,6 +14,7 @@
 LANES = 128
 WPB = 50
 FPB = 25
+BATCH = 20
 MESH = pl.DeviceIdType.MESH
 NT = (((1,), (1,)), ((), ()))
 
@@ -39,27 +40,31 @@
 
 
 def project(weighted, cols, profile, half):
-    head = weighted.astype(jnp.bfloat16)
-    tail = (weighted - head.astype(jnp.float32)).astype(jnp.bfloat16)
-    both = jnp.concatenate([head, tail], axis=0)
-    folded = lax.dot_general(cols, both, NT, preferred_element_type=jnp.float32)
-    folded = folded + pltpu.roll(folded, LANES // 2, 1)
-    return jnp.dot(
-        second_piece(folded, half),
-        jnp.concatenate([profile, profile], axis=0),
-        preferred_element_type=jnp.float32,
-    )
+    head = [g.astype(jnp.bfloat16) for g in weighted]
+    tail = [(g - h.astype(jnp.float32)).astype(jnp.bfloat16) for g, h in zip(weighted, head)]
+    both = [jnp.concatenate([h, t], axis=0) for h, t in zip(head, tail)]
+    folded = [
+        lax.dot_general(c, g, NT, preferred_element_type=jnp.float32) for c, g in zip(cols, both)
+    ]
+    folded = [f + pltpu.roll(f, LANES // 2, 1) for f in folded]
+    pieces = [second_piece(f, half) for f in folded]
+    return [
+        jnp.dot(f, jnp.concatenate([r, r], axis=0), preferred_element_type=jnp.float32)
+        for f, r in zip(pieces, profile)
+    ]
 
 
 def image_of(direction, cols, profile, half, quarter):
-    pieces = second_piece(direction, half)
-    pieces = jnp.concatenate([pieces, pieces], axis=0)
-    across = lax.dot_general(profile, pieces, NT, preferred_element_type=jnp.float32)
-    return jnp.dot(
-        second_piece(across, quarter),
-        jnp.concatenate([cols, cols], axis=0),
-        preferred_element_type=jnp.float32,
-    )
+    pieces = [second_piece(d, half) for d in direction]
+    pieces = [jnp.concatenate([d, d], axis=0) for d in pieces]
+    across = [
+        lax.dot_general(r, d, NT, preferred_element_type=jnp.float32) for r, d in zip(profile, pieces)
+    ]
+    pieces = [second_piece(u, quarter) for u in across]
+    return [
+        jnp.dot(u, jnp.concatenate([c, c], axis=0), preferred_element_type=jnp.float32)
+        for u, c in zip(pieces, cols)
+    ]
 
 
 def total(value):
@@ -102,41 +107,64 @@
             [jnp.where(keep, moved[0], moved[1]), jnp.where(keep, moved[1], moved[2])], axis=1
         )
 
-    for p in range(count):
-        row, col = row_off[p], col_off[p]
-        first_tile = col // LANES
-        shift = col - first_tile * LANES
-        weights = cut(1, first_tile, row, shift)
-        inverse[p] = weights
-        rhs = project(weights * cut(0, first_tile, row, shift), cols[p], profile[p], half)
-        direction[p] = rhs
-        residual[p] = rhs
-        spectra[p] = jnp.zeros_like(rhs)
-        norms[p] = jnp.broadcast_to(total(rhs * rhs), (8, LANES))
+    def start(ps):
+        weighted = []
+        for p in ps:
+            row, col = row_off[p], col_off[p]
+            first_tile = col // LANES
+            shift = col - first_tile * LANES
+            weights = cut(1, first_tile, row, shift)
+            inverse[p] = weights
+            weighted.append(weights * cut(0, first_tile, row, shift))
+        rhs = project(weighted, [cols[p] for p in ps], [profile[p] for p in ps], half)
+        for p, value in zip(ps, rhs):
+            direction[p] = value
+            residual[p] = value
+            spectra[p] = jnp.zeros_like(value)
+            norms[p] = jnp.broadcast_to(total(value * value), (8, LANES))
+
+    def sweep(ps):
+        c = [cols[p] for p in ps]
+        r = [profile[p] for p in ps]
+        along = [direction[p] for p in ps]
+        modeled = image_of(along, c, r, half, quarter)
+        imaged = project([inverse[p] * m for p, m in zip(ps, modeled)], c, r, half)
+        curvature = [total(d * q) for d, q in zip(along, imaged)]
+        now = [norms[p][0:1, 0:1] for p in ps]
+        size = [n / jnp.where(k > 0.0, k, 1.0) for n, k in zip(now, curvature)]
+        left = [residual[p] - a * q for p, a, q in zip(ps, size, imaged)]
+        later = [total(e * e) for e in left]
+        ratio = [n / jnp.where(b > 0.0, b, 1.0) for n, b in zip(later, now)]
+        for p, a, d, e, n, k in zip(ps, size, along, left, later, ratio):
+            spectra[p] += a * d
+            residual[p] = e
+            norms[p] = jnp.broadcast_to(n, (8, LANES))
+            direction[p] = e + k * d
+
+    def finish(ps):
+        c = [cols[p] for p in ps]
+        r = [profile[p] for p in ps]
+        along = [direction[p] for p in ps]
+        modeled = image_of(along, c, r, half, quarter)
+        curvature = [
+            2.0 * total(jnp.sum(inverse[p] * m * m, axis=0, keepdims=True)) for p, m in zip(ps, modeled)
+        ]
+        for p, d, k in zip(ps, along, curvature):
+            spectra[p] += norms[p][0:1, 0:1] / jnp.where(k > 0.0, k, 1.0) * d
+
+    sets = [list(range(first, first + BATCH)) for first in range(0, count, BATCH)]
+    for ps in sets:
+        start(ps)
     spectra[count] = jnp.zeros((32, LANES), jnp.float32)
 
-    def sweep(step, carry):
-        for p in range(count):
-            along = direction[p]
-            modeled = image_of(along, cols[p], profile[p], half, quarter)
-            imaged = project(inverse[p] * modeled, cols[p], profile[p], half)
-            curvature = total(along * imaged)
-            now = norms[p][0:1, 0:1]
-            size = now / jnp.where(curvature > 0.0, curvature, 1.0)
-            spectra[p] += size * along
-            left = residual[p] - size * imaged
-            residual[p] = left
-            later = total(left * left)
-            norms[p] = jnp.broadcast_to(later, (8, LANES))
-            direction[p] = left + later / jnp.where(now > 0.0, now, 1.0) * along
+    def step(index, carry):
+        for ps in sets:
+            sweep(ps)
         return carry
 
-    lax.fori_loop(0, ITERS - 1, sweep, 0)
-    for p in range(count):
-        along = direction[p]
-        modeled = image_of(along, cols[p], profile[p], half, quarter)
-        curvature = 2.0 * total(jnp.sum(inverse[p] * modeled * modeled, axis=0, keepdims=True))
-        spectra[p] += norms[p][0:1, 0:1] / jnp.where(curvature > 0.0, curvature, 1.0) * along
+    lax.fori_loop(0, ITERS - 1, step, 0)
+    for ps in sets:
+        finish(ps)
 
     for d in range(group):
         first = spectra[source[2 * d]]
@@ -227,19 +255,15 @@
 SMEM = pl.BlockSpec(memory_space=pltpu.SMEM)
 
 
-def local(exposure, row_prof, col_prof, row_off, col_off, dest, fibre_weight):
-    group = lax.axis_size("patch")
-    frames = lax.axis_size("frame")
-    count = dest.shape[1]
+def solve_call(count, group, row_off, col_off, dest, exposure, low, high, row_prof, col_prof, fibre_weight):
     f32 = jnp.float32
-    low, high = halo_rows(exposure, HALO)
-    profile = jnp.swapaxes(row_prof[0], 1, 2)
+    profile = jnp.swapaxes(row_prof, 1, 2)
     profile = jnp.pad(profile, ((0, 0), (0, 0), (0, LANES // 2 - WPB)))
     profile = jnp.concatenate([profile, profile], axis=2)
-    cols = jnp.pad(col_prof[0], ((0, 0), (0, 32 - FPB), (0, 0)))
-    weight = jnp.pad(fibre_weight[0].T, ((0, 32 - FPB), (0, LANES - count)))
-    tiles = exposure.shape[3] // LANES
-    send, contrib = pl.pallas_call(
+    cols = jnp.pad(col_prof, ((0, 0), (0, 32 - FPB), (0, 0)))
+    weight = jnp.pad(fibre_weight.T, ((0, 32 - FPB), (0, LANES - count)))
+    tiles = exposure.shape[2] // LANES
+    return pl.pallas_call(
         functools.partial(solve_kernel, count, group),
         out_shape=(
             jax.ShapeDtypeStruct((group, FPB, LANES), f32),
@@ -259,7 +283,18 @@
         ],
         compiler_params=pltpu.CompilerParams(vmem_limit_bytes=40 << 20),
         name="solve",
-    )(row_off[0], col_off[0], dest[0], exposure[0], low, high, profile, cols, weight)
+    )(row_off, col_off, dest, exposure, low, high, profile, cols, weight)
+
+
+def local(exposure, row_prof, col_prof, row_off, col_off, dest, fibre_weight):
+    group = lax.axis_size("patch")
+    frames = lax.axis_size("frame")
+    count = dest.shape[1]
+    f32 = jnp.float32
+    low, high = halo_rows(exposure, HALO)
+    send, contrib = solve_call(
+        count, group, row_off[0], col_off[0], dest[0], exposure[0], low, high,
+        row_prof[0], col_prof[0], fibre_weight[0])
     chips = frames // 2
     recv, sums = pl.pallas_call(
         functools.partial(exchange_kernel, group, frames),

time: 110 us -> 58.3 us (0.53)
  Pallas kernels: 97.2 us -> 45.8 us
    pallas_call x1, Pallas kernels: 61.5 us -> 10.2 us  [solve_call(): pl.pallas_call(functools.partial(solve_kernel, count, group), out_shape=(...]
where the time goes in v2:
time: 58.3 us; the launch traced here: 57.5 us
  Pallas kernels  45.8 us (79%)
  starting transfers between devices  5.95 us (10%)
  local copies, waits for them, and re-layouts  4.38 us (8%)
  between operations  0.76 us (1%)
    pallas_call x1, Pallas kernels, local(): pl.pallas_call(functools.partial(exchange_kernel, group, frames), out_sha...  32 us
    pallas_call x1, Pallas kernels, solve_call(): pl.pallas_call(functools.partial(solve_kernel, count, group), out_shape=(...  10.2 us
    ppermute x1, starting transfers between devices, halo_rows(): lax.ppermute(lax.slice_in_dim(block, rows - width, None, axis=2), axes, f...  4.65 us
    pallas_call x1, Pallas kernels, local(): pl.pallas_call(functools.partial(format_kernel, count, group), out_shape=...  3.61 us
    unnamed x21, local copies, waits for them, and re-layouts  3.24 us
    ppermute x1, starting transfers between devices, halo_rows(): lax.ppermute(lax.slice_in_dim(block, 0, width, axis=2), axes, backward)  1.29 us
  transfers between devices with their start and end apart: 2, of which 1 were waited for; matrix products, arithmetic and copies ran while one was open for 1% of the time, Pallas kernels for 0%

profile of v2, /device:TPU:1, one launch (start us, length us, event | category | flops | bytes accessed | tf_op | source)
XLA Modules:
  0.0 57.5 jit_solution(15443785517551681558)
XLA Ops:
  0.6 0.0 copy-start.7
  0.6 0.0 copy-start.8
  0.6 1.0 %fusion = (bf16[1,2,8,4096]{3,2,1,0:T(8,128)(2,1)S(1)}, bf16[1,2,8,4096]{3,2,1,0:T(8,128)(2,1)S(1)}) fusion(bf16[1,2,56,4096]{3,2,1,0:T(8,128)(2,1)} %param.7), kind=kLoop, calls=%fused_computation.2 | loop fusion | bytes 524288 | tf_op jit(solution)/shard_map/slice | solution.py:29
  1.7 1.3 %collective-permute-start.1 = (bf16[1,2,8,4096]{3,2,1,0:T(8,128)(2,1)S(1)}, bf16[1,2,8,4096]{3,2,1,0:T(8,128)(2,1)S(1)}, u32[]{:S(2)}, u32[]{:S(2)}) collective-permute-start(bf16[1,2,8,4096]{3,2,1,0:T(8,128)(2,1)S(1)} %get-tuple-element.14), channel_id=1, source_target_pairs={{1,0},{2,1},{3,2},{4,3},{5,4},{6,5},{7,6},{8,7},{9,8},{10,9},{11,1... | collective-permute-start | bytes 393224 | tf_op jit(solution)/shard_map/ppermute | solution.py:29
  3.0 4.7 %collective-permute-start = (bf16[1,2,8,4096]{3,2,1,0:T(8,128)(2,1)S(1)}, bf16[1,2,8,4096]{3,2,1,0:T(8,128)(2,1)S(1)}, u32[]{:S(2)}, u32[]{:S(2)}) collective-permute-start(bf16[1,2,8,4096]{3,2,1,0:T(8,128)(2,1)S(1)} %get-tuple-element.15), channel_id=1, source_target_pairs={{0,1},{1,2},{2,3},{3,4},{4,5},{5,6},{6,7},{7,8},{8,9},{9,10},{10,1... | collective-permute-start | bytes 393224 | tf_op jit(solution)/shard_map/ppermute | solution.py:28
  7.6 0.0 copy-done.8
  7.7 0.1 copy.11
  7.8 0.0 copy-done.7
  7.8 0.0 copy-start.6
  7.8 0.2 copy.9
  8.0 0.7 %copy-done.6 = bf16[1,20,25,256]{3,1,2,0:T(8,128)(2,1)S(1)} copy-done((bf16[1,20,25,256]{3,1,2,0:T(8,128)(2,1)S(1)}, bf16[1,20,25,256]{3,1,2,0:T(8,128)(2,1)}, u32[]{:S(2)}) %copy-start.6) | copy-done | bytes 256024
  8.7 0.1 copy.13
  8.8 0.0 copy-start
  8.8 0.1 pad.12
  8.9 0.2 pad_maximum_fusion.profile
  9.1 0.0 collective-permute-done.1
  9.1 0.4 collective-permute-done
  9.6 0.0 copy-start.3
  9.6 0.0 copy-start.4
  9.6 0.0 copy-start.5
  9.6 0.4 copy-done
  10.0 0.3 copy-done.3
  10.3 0.0 copy-done.4
  10.3 0.0 copy-done.5
  10.3 10.2 %solve.1 = (f32[16,25,128]{2,1,0:T(8,128)S(1)}, f32[2,128,128]{2,1,0:T(8,128)S(1)}) custom-call(s32[20]{0:T(128)S(1)} %bitcast.22, s32[20]{0:T(128)S(1)} %bitcast.23, s32[20]{0:T(128)S(1)} %bitcast.24, bf16[2,56,4096]{2,1,0:T(8,128)(2,1)S(1)} %bitcast.19, bf16[2,8,4096]{2,1,0:T(8,128)(2,1)S(1)} %bitcast.21, bf16[2,8,4096]{2,1,0:T(8,128)(2,1)S(1)} %bitcast.20, ...), custom_call_target="tpu_custom_call" | custom-call | tf_op jit(solution)/shard_map/solve/pallas_call | solution.py:266
  20.5 0.0 copy-start.1
  20.5 0.7 %copy-done.1 = f32[16,25,128]{2,1,0:T(8,128)} copy-done((f32[16,25,128]{2,1,0:T(8,128)}, f32[16,25,128]{2,1,0:T(8,128)S(1)}, u32[]{:S(2)}) %copy-start.1) | copy-done | bytes 204824
  21.2 0.0 copy-start.2
  21.2 0.7 %copy-done.2 = f32[2,128,128]{2,1,0:T(8,128)} copy-done((f32[2,128,128]{2,1,0:T(8,128)}, f32[2,128,128]{2,1,0:T(8,128)S(1)}, u32[]{:S(2)}) %copy-start.2) | copy-done | bytes 131096
  21.9 32.0 %exchange.1 = (f32[16,25,128]{2,1,0:T(8,128)}, f32[2,128,128]{2,1,0:T(8,128)}) custom-call(f32[16,25,128]{2,1,0:T(8,128)} %copy-done.1, f32[2,128,128]{2,1,0:T(8,128)} %copy-done.2), custom_call_target="tpu_custom_call" | custom-call | tf_op jit(solution)/shard_map/exchange/pallas_call | solution.py:299
  53.9 3.6 %arrange.1 = (f32[25,32,50]{2,1,0:T(8,128)}, f32[25,20,50]{2,1,0:T(8,128)}) custom-call(f32[16,25,128]{2,1,0:T(8,128)} %get-tuple-element.10.recv, f32[2,128,128]{2,1,0:T(8,128)} %get-tuple-element.11.sums), custom_call_target="tpu_custom_call" | custom-call | tf_op jit(solution)/shard_map/arrange/pallas_call | solution.py:320
  (2 shorter events, 0.0 us)
Async XLA Ops:
  0.6 7.1 %copy-start.7 = (bf16[1,20,50,64]{3,2,1,0:T(8,128)(2,1)S(1)}, bf16[1,20,50,64]{3,2,1,0:T(8,128)(2,1)}, u32[]{:S(2)}) copy-start(bf16[1,20,50,64]{3,2,1,0:T(8,128)(2,1)} %param.8) | copy-start | bytes 384004
  0.6 7.0 %copy-start.8 = (f32[1,20,25]{2,0,1:T(1,128)S(1)}, f32[1,20,25]{2,0,1:T(1,128)}, u32[]{:S(2)}) copy-start(f32[1,20,25]{2,0,1:T(1,128)} %param.13) | copy-start | bytes 6004
  1.7 7.4 %collective-permute-start.1 = (bf16[1,2,8,4096]{3,2,1,0:T(8,128)(2,1)S(1)}, bf16[1,2,8,4096]{3,2,1,0:T(8,128)(2,1)S(1)}, u32[]{:S(2)}, u32[]{:S(2)}) collective-permute-start(bf16[1,2,8,4096]{3,2,1,0:T(8,128)(2,1)S(1)} %get-tuple-element.14), channel_id=1, source_target_pairs={{1,0},{2,1},{3,2},{4,3},{5,4},{6,5},{7,6},{8,7},{9,8},{10,9},{11,1... | collective-permute-start | bytes 393224 | tf_op jit(solution)/shard_map/ppermute | solution.py:29
  3.0 6.6 %collective-permute-start = (bf16[1,2,8,4096]{3,2,1,0:T(8,128)(2,1)S(1)}, bf16[1,2,8,4096]{3,2,1,0:T(8,128)(2,1)S(1)}, u32[]{:S(2)}, u32[]{:S(2)}) collective-permute-start(bf16[1,2,8,4096]{3,2,1,0:T(8,128)(2,1)S(1)} %get-tuple-element.15), channel_id=1, source_target_pairs={{0,1},{1,2},{2,3},{3,4},{4,5},{5,6},{6,7},{7,8},{8,9},{9,10},{10,1... | collective-permute-start | bytes 393224 | tf_op jit(solution)/shard_map/ppermute | solution.py:28
  7.8 1.0 %copy-start.6 = (bf16[1,20,25,256]{3,1,2,0:T(8,128)(2,1)S(1)}, bf16[1,20,25,256]{3,1,2,0:T(8,128)(2,1)}, u32[]{:S(2)}) copy-start(bf16[1,20,25,256]{3,1,2,0:T(8,128)(2,1)} %param.9) | copy-start | bytes 768004
  8.8 1.2 %copy-start = (bf16[1,2,56,4096]{3,2,1,0:T(8,128)(2,1)S(1)}, bf16[1,2,56,4096]{3,2,1,0:T(8,128)(2,1)}, u32[]{:S(2)}) copy-start(bf16[1,2,56,4096]{3,2,1,0:T(8,128)(2,1)} %param.7) | copy-start | bytes 2752516
  9.6 0.7 %copy-start.3 = (s32[1,20]{1,0:T(1,128)S(1)}, s32[1,20]{1,0:T(1,128)}, u32[]{:S(2)}) copy-start(s32[1,20]{1,0:T(1,128)} %param.10) | copy-start | bytes 244
  9.6 0.7 %copy-start.4 = (s32[1,20]{1,0:T(1,128)S(1)}, s32[1,20]{1,0:T(1,128)}, u32[]{:S(2)}) copy-start(s32[1,20]{1,0:T(1,128)} %param.11) | copy-start | bytes 244
  9.6 0.8 %copy-start.5 = (s32[1,20]{1,0:T(1,128)S(1)}, s32[1,20]{1,0:T(1,128)}, u32[]{:S(2)}) copy-start(s32[1,20]{1,0:T(1,128)} %param.12) | copy-start | bytes 244
  20.5 0.7 %copy-start.1 = (f32[16,25,128]{2,1,0:T(8,128)}, f32[16,25,128]{2,1,0:T(8,128)S(1)}, u32[]{:S(2)}) copy-start(f32[16,25,128]{2,1,0:T(8,128)S(1)} %get-tuple-element.8.send) | copy-start | bytes 614404
  21.2 0.7 %copy-start.2 = (f32[2,128,128]{2,1,0:T(8,128)}, f32[2,128,128]{2,1,0:T(8,128)S(1)}, u32[]{:S(2)}) copy-start(f32[2,128,128]{2,1,0:T(8,128)S(1)} %get-tuple-element.9.contrib) | copy-start | bytes 393220

commit v3 on v0

v3 whole, which is shorter than its diff:
```python
import functools

import jax
import jax.numpy as jnp
from jax import lax
from jax.experimental import pallas as pl
from jax.experimental.pallas import tpu as pltpu
from jax.sharding import PartitionSpec as P

HALO = 8
PC = 256
ITERS = 6
PR = 64
LANES = 128
WPB = 50
FPB = 25
MESH = pl.DeviceIdType.MESH
NT = (((1,), (1,)), ((), ()))


def lane_index(shape):
    return lax.broadcasted_iota(jnp.int32, shape, len(shape) - 1)


def second_piece(value, first):
    head = value.astype(jnp.bfloat16).astype(jnp.float32)
    return jnp.where(first, value, value - head).astype(jnp.bfloat16)


def project(weighted, cols, profile, half):
    head = [g.astype(jnp.bfloat16) for g in weighted]
    tail = [(g - h.astype(jnp.float32)).astype(jnp.bfloat16) for g, h in zip(weighted, head)]
    both = [jnp.concatenate([h, t], axis=0) for h, t in zip(head, tail)]
    folded = [
        lax.dot_general(c, g, NT, preferred_element_type=jnp.float32) for c, g in zip(cols, both)
    ]
    folded = [f + pltpu.roll(f, LANES // 2, 1) for f in folded]
    pieces = [second_piece(f, half) for f in folded]
    return [
        jnp.dot(f, jnp.concatenate([r, r], axis=0), preferred_element_type=jnp.float32)
        for f, r in zip(pieces, profile)
    ]


def image_of(direction, cols, profile, half, quarter):
    pieces = [second_piece(d, half) for d in direction]
    pieces = [jnp.concatenate([d, d], axis=0) for d in pieces]
    across = [
        lax.dot_general(r, d, NT, preferred_element_type=jnp.float32) for r, d in zip(profile, pieces)
    ]
    pieces = [second_piece(u, quarter) for u in across]
    return [
        jnp.dot(u, jnp.concatenate([c, c], axis=0), preferred_element_type=jnp.float32)
        for u, c in zip(pieces, cols)
    ]


def total(value):
    return jnp.sum(jnp.sum(value, axis=0, keepdims=True), axis=1, keepdims=True)


def solve_kernel(
    count, group, frames,
    row_off, col_off, dest, exposure, row_prof, col_prof, fibre_weight,
    ext_out, coadd_out,
    pixels, rows_raw, cols_raw, weight_raw, low, high, ext, cols_wide, profile, cols,
    cut_weight, cut_value, inverse, direction, residual, spectra, norms, send, recv, contrib,
    arrived, mine, parts, sums,
    load_sem, halo_out, halo_in, swap_sem, out_sem, in_sem, part_out, part_in, sum_out, sum_in, fwd_out, fwd_in,
):
    f32 = jnp.float32
    section = lax.axis_index("section")
    frame = lax.axis_index("frame")
    me = lax.axis_index("patch")
    sections = lax.axis_size("section")
    core = lax.rem(frame, 2)
    chip = frame // 2
    chips = frames // 2
    partner = frame + 1 - 2 * core
    band = section * group + me
    bands = sections * group
    above = lax.rem(band + bands - 1, bands)
    below = lax.rem(band + 1, bands)

    def at_band(index):
        return {"section": index // group, "patch": lax.rem(index, group)}

    barrier = pltpu.get_barrier_semaphore()
    inner = [{"patch": lax.rem(me + k, group)} for k in range(1, group)]
    peers = [{"frame": lax.rem(frame + 2 * k, frames)} for k in range(1, chips)]
    partners = [at_band(above), at_band(below)] + [{"frame": partner}] + peers + inner
    for device in partners:
        pl.semaphore_signal(barrier, inc=1, device_id=device, device_id_type=MESH)
    loads = [
        pltpu.make_async_copy(source, target, load_sem.at[i])
        for i, (source, target) in enumerate(
            [(exposure, pixels), (row_prof, rows_raw), (col_prof, cols_raw), (fibre_weight, weight_raw)]
        )
    ]
    for load in loads:
        load.start()
    pl.semaphore_wait(barrier, len(partners))

    depth = exposure.shape[1]
    down = pltpu.make_async_remote_copy(
        exposure.at[:, depth - HALO:depth, :], low, halo_out.at[0], halo_in.at[0],
        device_id=at_band(below), device_id_type=MESH)
    up = pltpu.make_async_remote_copy(
        exposure.at[:, 0:HALO, :], high, halo_out.at[1], halo_in.at[1],
        device_id=at_band(above), device_id_type=MESH)
    down.start()
    up.start()

    half = lane_index((32, LANES)) < LANES // 2
    quarter = lane_index((PR, PR)) < PR // 2
    tiles = exposure.shape[2] // LANES

    loads[1].wait()
    for p in range(count):
        turned = jnp.pad(rows_raw[p].astype(f32), ((0, PR - WPB), (0, LANES - PR))).T[0:PR]
        profile[p] = jnp.concatenate([turned, turned], axis=1).astype(jnp.bfloat16)
    loads[2].wait()
    stride = cols_wide.shape[1] // FPB
    for k in range(FPB):
        for j in range(2):
            cols_wide[j, k * stride:k * stride + count, :] = (
                cols_raw[k, :, j * LANES:(j + 1) * LANES].astype(f32))
    gap = jnp.zeros((32 - FPB, PC), f32)
    for p in range(count):
        taken = [cols_wide[j, pl.ds(p, FPB, stride=stride), :] for j in range(2)]
        cols[p] = jnp.concatenate([jnp.concatenate(taken, axis=1), gap], axis=0).astype(jnp.bfloat16)

    loads[0].wait()
    for channel in range(2):
        for tile in range(tiles):
            at = slice(tile * LANES, (tile + 1) * LANES)
            ext[channel, tile, HALO:PR, :] = pixels[channel, :, at].astype(f32)

    starts = [row_off[p] for p in range(count)]
    columns = [col_off[p] for p in range(count)]
    firsts = [c // LANES for c in columns]
    shifts = [c - t * LANES for c, t in zip(columns, firsts)]

    def cut(first, size):
        lanes = lane_index((size, LANES))
        for p in range(count):
            keep = lanes < LANES - shifts[p]
            moved = [
                [
                    pltpu.roll(ext[channel, firsts[p] + j, first:first + size, :], LANES - shifts[p], 1)
                    for j in range(3)
                ]
                for channel in range(2)
            ]
            for j in range(2):
                value, weight = [jnp.where(keep, m[j], m[j + 1]) for m in moved]
                cut_weight[p, j, first:first + size, :] = weight
                cut_value[p, j, first:first + size, :] = weight * value

    cut(HALO, PR - HALO)
    loads[3].wait()
    raw = jnp.concatenate([weight_raw[...], jnp.zeros((count, LANES - FPB), f32)], axis=1)
    weights = jnp.concatenate([raw, jnp.zeros((LANES - count, LANES), f32)], axis=0).T[0:32]

    source = []
    for d in range(group):
        first = jnp.int32(count)
        last = jnp.int32(count)
        for p in range(count):
            last = jnp.where(dest[p] == d, p, last)
            first = jnp.where(dest[count - 1 - p] == d, count - 1 - p, first)
        source.append((first, jnp.where(last == first, count, last)))

    down.wait_recv()
    up.wait_recv()
    for channel in range(2):
        for tile in range(tiles):
            at = slice(tile * LANES, (tile + 1) * LANES)
            ext[channel, tile, 0:HALO, :] = jnp.where(band > 0, low[channel, :, at].astype(f32), 0.0)
            ext[channel, tile, PR:PR + HALO, :] = jnp.where(
                band < bands - 1, high[channel, :, at].astype(f32), 0.0)
    cut(0, HALO)
    cut(PR, HALO)

    every = list(range(count))
    c = [cols[p] for p in every]
    r = [profile[p] for p in every]
    weighted = []
    for p in every:
        inverse[p] = jnp.concatenate([cut_weight[p, j, pl.ds(starts[p], PR), :] for j in range(2)], axis=1)
        weighted.append(
            jnp.concatenate([cut_value[p, j, pl.ds(starts[p], PR), :] for j in range(2)], axis=1))
    for p, value in zip(every, project(weighted, c, r, half)):
        direction[p] = value
        residual[p] = value
        spectra[p] = jnp.zeros_like(value)
        norms[p] = jnp.broadcast_to(total(value * value), (8, LANES))
    spectra[count] = jnp.zeros((32, LANES), f32)

    def sweep(index, carry):
        c = [cols[p] for p in every]
        r = [profile[p] for p in every]
        along = [direction[p] for p in every]
        modeled = image_of(along, c, r, half, quarter)
        imaged = project([inverse[p] * m for p, m in zip(every, modeled)], c, r, half)
        curvature = [total(d * q) for d, q in zip(along, imaged)]
        now = [norms[p][0:1, 0:1] for p in every]
        size = [n / jnp.where(k > 0.0, k, 1.0) for n, k in zip(now, curvature)]
        left = [residual[p] - a * q for p, a, q in zip(every, size, imaged)]
        later = [total(e * e) for e in left]
        ratio = [n / jnp.where(b > 0.0, b, 1.0) for n, b in zip(later, now)]
        for p, a, d, e, n, k in zip(every, size, along, left, later, ratio):
            spectra[p] += a * d
            residual[p] = e
            norms[p] = jnp.broadcast_to(n, (8, LANES))
            direction[p] = e + k * d
        return carry

    lax.fori_loop(0, ITERS - 1, sweep, 0)
    along = [direction[p] for p in every]
    modeled = image_of(along, [cols[p] for p in every], [profile[p] for p in every], half, quarter)
    curvature = [
        2.0 * total(jnp.sum(inverse[p] * m * m, axis=0, keepdims=True)) for p, m in zip(every, modeled)
    ]
    for p, d, k in zip(every, along, curvature):
        spectra[p] += norms[p][0:1, 0:1] / jnp.where(k > 0.0, k, 1.0) * d

    pairs = count // 2
    per_half = pairs // 2
    marked = lane_index((32, LANES)) % (LANES // 2) == WPB
    for j in range(pairs):
        scale = jnp.where(
            half,
            jnp.broadcast_to(weights[:, j:j + 1], (32, LANES)),
            jnp.broadcast_to(weights[:, pairs + j:pairs + j + 1], (32, LANES)))
        value = scale * jnp.where(marked, 1.0, jnp.where(half, spectra[j], spectra[pairs + j]))
        start = (j % per_half) * FPB
        contrib[j // per_half, start:start + FPB, :] = value[0:FPB]
    for h in range(2):
        contrib[h, per_half * FPB:, :] = jnp.zeros((LANES - per_half * FPB, LANES), f32)
    swap = pltpu.make_async_remote_copy(
        contrib.at[1 - core], arrived, swap_sem.at[0], swap_sem.at[1],
        device_id={"frame": partner}, device_id_type=MESH)
    swap.start()
    for d in range(group):
        send[d] = jnp.where(half, spectra[source[d][0]], spectra[source[d][1]])[0:FPB]
    spread = []
    for k in range(1, group):
        to = lax.rem(me + k, group)
        spread.append(pltpu.make_async_remote_copy(
            send.at[to], recv.at[me], out_sem.at[k], in_sem.at[k],
            device_id={"patch": to}, device_id_type=MESH))
        spread[-1].start()

    def chunk(index):
        return pl.ds(pl.multiple_of(index * 32, 32), 32)

    swap.wait()
    mine[...] = contrib[core] + arrived[...]
    scatter = []
    for k in range(1, chips):
        to = lax.rem(chip + k, chips)
        scatter.append(pltpu.make_async_remote_copy(
            mine.at[chunk(to)], parts.at[chip], part_out.at[k], part_in.at[k],
            device_id={"frame": 2 * to + core}, device_id_type=MESH))
        scatter[-1].start()
    parts[chip] = mine[chunk(chip), :]
    recv[me] = send[me]
    for copy in scatter:
        copy.wait_recv()
    whole = parts[0]
    for k in range(1, chips):
        whole = whole + parts[k]
    sums[core, chunk(chip), :] = whole
    gather = []
    for k in range(1, chips):
        to = lax.rem(chip + k, chips)
        gather.append(pltpu.make_async_remote_copy(
            sums.at[core, chunk(chip)], sums.at[core, chunk(chip)], sum_out.at[k], sum_in.at[k],
            device_id={"frame": 2 * to + core}, device_id_type=MESH))
        gather[-1].start()
    forward = []
    for k in range(chips):
        from_chip = lax.rem(chip + chips - k, chips)
        if k:
            gather[k - 1].wait_recv()
        forward.append(pltpu.make_async_remote_copy(
            sums.at[core, chunk(from_chip)], sums.at[core, chunk(from_chip)], fwd_out.at[k], fwd_in.at[k],
            device_id={"frame": partner}, device_id_type=MESH))
        forward[-1].start()

    for copy in spread:
        copy.wait_recv()
    for k in range(FPB):
        rows = recv[:, k, :]
        ext_out[k, pl.ds(0, group, stride=2), :] = rows[:, 0:WPB]
        ext_out[k, pl.ds(1, group, stride=2), :] = pltpu.roll(rows, LANES // 2, 1)[:, 0:WPB]
    for copy in forward:
        copy.wait_recv()
    for k in range(FPB):
        for h in range(2):
            rows = sums[h, pl.ds(k, per_half, stride=FPB), :]
            for s in range(2):
                here = rows if s == 0 else pltpu.roll(rows, LANES // 2, 1)
                start = s * pairs + h * per_half
                coadd_out[k, start:start + per_half, :] = here[:, 0:WPB] / here[:, WPB:WPB + 1]
    down.wait_send()
    up.wait_send()
    swap_done = scatter + gather + forward + spread
    for copy in swap_done:
        copy.wait_send()


VMEM = pl.BlockSpec(memory_space=pltpu.VMEM)
SMEM = pl.BlockSpec(memory_space=pltpu.SMEM)
ANY = pl.BlockSpec(memory_space=pl.ANY)


def local(exposure, row_prof, col_prof, row_off, col_off, dest, fibre_weight):
    group = lax.axis_size("patch")
    frames = lax.axis_size("frame")
    count = dest.shape[1]
    chips = frames // 2
    f32, bf16 = jnp.float32, jnp.bfloat16
    _, channels, depth, width = exposure.shape
    tiles = width // LANES
    stride = -(-count // 8) * 8
    ext_out, coadd_out = pl.pallas_call(
        functools.partial(solve_kernel, count, group, frames),
        out_shape=(
            jax.ShapeDtypeStruct((FPB, 2 * group, WPB), f32),
            jax.ShapeDtypeStruct((FPB, count, WPB), f32),
        ),
        in_specs=[SMEM] * 3 + [ANY] * 4,
        out_specs=(VMEM, VMEM),
        scratch_shapes=[
            pltpu.VMEM((channels, depth, width), bf16),
            pltpu.VMEM((count, WPB, PR), bf16),
            pltpu.VMEM((FPB, count, PC), bf16),
            pltpu.VMEM((count, FPB), f32),
            pltpu.VMEM((channels, HALO, width), bf16),
            pltpu.VMEM((channels, HALO, width), bf16),
            pltpu.VMEM((channels, tiles + 1, PR + HALO, LANES), f32),
            pltpu.VMEM((2, FPB * stride, LANES), f32),
            pltpu.VMEM((count, PR, LANES), bf16),
            pltpu.VMEM((count, 32, PC), bf16),
            pltpu.VMEM((count, 2, PR + HALO, LANES), f32),
            pltpu.VMEM((count, 2, PR + HALO, LANES), f32),
            pltpu.VMEM((count, PR, PC), f32),
            pltpu.VMEM((count, 32, LANES), f32),
            pltpu.VMEM((count, 32, LANES), f32),
            pltpu.VMEM((count + 1, 32, LANES), f32),
            pltpu.VMEM((count, 8, LANES), f32),
            pltpu.VMEM((group, FPB, LANES), f32),
            pltpu.VMEM((group, FPB, LANES), f32),
            pltpu.VMEM((2, LANES, LANES), f32),
            pltpu.VMEM((LANES, LANES), f32),
            pltpu.VMEM((LANES, LANES), f32),
            pltpu.VMEM((chips, 32, LANES), f32),
            pltpu.VMEM((2, LANES, LANES), f32),
            pltpu.SemaphoreType.DMA((4,)),
            pltpu.SemaphoreType.DMA((2,)),
            pltpu.SemaphoreType.DMA((2,)),
            pltpu.SemaphoreType.DMA((2,)),
            pltpu.SemaphoreType.DMA((group,)),
            pltpu.SemaphoreType.DMA((group,)),
            pltpu.SemaphoreType.DMA((chips,)),
            pltpu.SemaphoreType.DMA((chips,)),
            pltpu.SemaphoreType.DMA((chips,)),
            pltpu.SemaphoreType.DMA((chips,)),
            pltpu.SemaphoreType.DMA((chips,)),
            pltpu.SemaphoreType.DMA((chips,)),
        ],
        compiler_params=pltpu.CompilerParams(
            collective_id=0, has_side_effects=True, vmem_limit_bytes=48 << 20),
        name="solve",
    )(
        row_off[0], col_off[0], dest[0], exposure[0], row_prof[0],
        jnp.swapaxes(col_prof[0], 0, 1), fibre_weight[0],
    )
    return jnp.transpose(ext_out, (1, 2, 0))[None], jnp.transpose(coadd_out, (1, 2, 0))


def solution(mesh):
    in_specs = (
        P("frame", None, ("section", "patch"), None),
        P("frame", ("section", "patch"), None, None),
        P("frame", ("section", "patch"), None, None),
        P("frame", ("section", "patch")),
        P("frame", ("section", "patch")),
        P("frame", ("section", "patch")),
        P("frame", ("section", "patch"), None),
    )
    out_specs = (P("frame", ("section", "patch"), None, None), P(("section", "patch"), None, None))
    return jax.shard_map(local, mesh=mesh, in_specs=in_specs, out_specs=out_specs, check_vma=False)
```

time: 184 us -> 51.4 us (0.28)
  Pallas kernels: 0 us -> 44.5 us
  local copies, waits for them, and re-layouts: 49 us -> 5.95 us
  waiting for transfers between devices: 42.1 us -> 0 us
  blocking collectives: 31.2 us -> 0 us
  matrix products: 20.4 us -> 0 us
  starting transfers between devices: 15.7 us -> 0 us
  between operations: 14.4 us -> 0.66 us
  other arithmetic: 10.1 us -> 0 us
    pallas_call x0 -> x1, Pallas kernels: none -> 44.5 us  [local(): pl.pallas_call(functools.partial(solve_kernel, count, group, frames), out...]
    gather x65 -> x0, local copies, waits for them, and re-layouts: 43.1 us -> none
    psum x1 -> x0, waiting for transfers between devices: 41.7 us -> none  [local(): totals = lax.psum((numerator, denominator), 'frame')]
    psum x1 -> x0, blocking collectives: 31.2 us -> none  [local(): totals = lax.psum((numerator, denominator), 'frame')]
    dot_general x26 -> x0, matrix products: 20.4 us -> none  [the longest x6 5.32 us: solve_batch(): jnp.einsum('...wr,...wc->...rc', row_float, across, precision=highest)]
    all_to_all x1 -> x0, starting transfers between devices: 10.3 us -> none  [local(): lax.all_to_all(picked * weight_mask, 'patch', split_axis=1, concat_axis=1...]
    ppermute x2 -> x0, starting transfers between devices: 5.32 us -> none  [the longest x1 4.03 us: padded(): lax.ppermute(lax.slice_in_dim(block, block.shape[dim] - width, None, axis...]
    reduce_sum x7 -> x0, other arithmetic: 3.03 us -> none  [the longest x5 1.67 us: solve_batch(): norm_next = jnp.sum(residual * residual, axis=(-2, -1), keepdims=True)]
  transfers between devices with their start and end apart: 4 -> 0, of which waited for: 2 -> 0; matrix products, arithmetic and copies ran while one was open for 4% -> 0% of each run, Pallas kernels for 0% -> 0%
where the time goes in v3:
time: 51.4 us; the launch traced here: 51.1 us
  Pallas kernels  44.5 us (87%)
  local copies, waits for them, and re-layouts  5.95 us (12%)
  between operations  0.66 us (1%)
    pallas_call x1, Pallas kernels, local(): pl.pallas_call(functools.partial(solve_kernel, count, group, frames), out...  44.5 us
    unnamed x17, local copies, waits for them, and re-layouts  5.95 us

profile of v3, /device:TPU:1, one launch (start us, length us, event | category | flops | bytes accessed | tf_op | source)
XLA Modules:
  0.0 51.1 jit_solution(17967703808412838476)
XLA Ops:
  0.6 0.0 copy-start.6
  0.6 0.7 %copy-done.6 = f32[1,20,25]{2,0,1:T(1,128)S(1)} copy-done((f32[1,20,25]{2,0,1:T(1,128)S(1)}, f32[1,20,25]{2,0,1:T(1,128)}, u32[]{:S(2)}) %copy-start.6) | copy-done | bytes 2024
  1.3 0.0 copy-start.3
  1.3 0.0 copy-start.4
  1.3 0.0 copy-start.5
  1.3 0.6 %copy-done.3 = s32[1,20]{1,0:T(1,128)S(1)} copy-done((s32[1,20]{1,0:T(1,128)S(1)}, s32[1,20]{1,0:T(1,128)}, u32[]{:S(2)}) %copy-start.3) | copy-done | bytes 104
  2.0 0.0 copy-done.4
  2.0 0.0 copy-done.5
  2.0 0.0 copy-start
  2.0 1.2 %copy-done = bf16[1,2,56,4096]{3,2,1,0:T(8,128)(2,1)S(1)} copy-done((bf16[1,2,56,4096]{3,2,1,0:T(8,128)(2,1)S(1)}, bf16[1,2,56,4096]{3,2,1,0:T(8,128)(2,1)}, u32[]{:S(2)}) %copy-start) | copy-done | bytes 917528
  3.2 0.0 copy-start.1
  3.2 1.0 %copy-done.1 = bf16[1,20,25,256]{3,1,2,0:T(8,128)(2,1)S(1)} copy-done((bf16[1,20,25,256]{3,1,2,0:T(8,128)(2,1)S(1)}, bf16[1,20,25,256]{3,1,2,0:T(8,128)(2,1)}, u32[]{:S(2)}) %copy-start.1) | copy-done | bytes 256024
  4.2 0.0 copy-start.2
  4.2 1.0 %copy-done.2 = bf16[1,20,50,64]{3,2,1,0:T(8,128)(2,1)S(1)} copy-done((bf16[1,20,50,64]{3,2,1,0:T(8,128)(2,1)S(1)}, bf16[1,20,50,64]{3,2,1,0:T(8,128)(2,1)}, u32[]{:S(2)}) %copy-start.2) | copy-done | bytes 128024
  5.1 44.5 %solve.1 = (f32[25,32,50]{2,1,0:T(8,128)S(1)}, f32[25,20,50]{2,1,0:T(8,128)S(1)}) custom-call(s32[20]{0:T(128)S(1)} %bitcast.21, s32[20]{0:T(128)S(1)} %bitcast.22, s32[20]{0:T(128)S(1)} %bitcast.23, bf16[2,56,4096]{2,1,0:T(8,128)(2,1)S(1)} %bitcast.15, bf16[20,50,64]{2,1,0:T(8,128)(2,1)S(1)} %bitcast.19, bf16[25,20,256]{2,1,0:T(8,128)(2,1)S(1)} %bitcast.17, ...), custom_call_target="tpu_custom_call" | custom-call | tf_op jit(solution)/shard_map/solve/pallas_call | solution.py:328
  49.6 0.8 %copy.14 = f32[1,32,50,25]{2,1,3,0:T(8,128)} copy(f32[1,32,50,25]{2,1,3,0:T(8,128)S(1)} %bitcast.16) | data formatting | bytes 320000
  50.4 0.7 %copy.15 = f32[20,50,25]{1,0,2:T(8,128)} copy(f32[20,50,25]{1,0,2:T(8,128)S(1)} %bitcast.18) | data formatting | bytes 200000
  (1 shorter events, 0.0 us)
Async XLA Ops:
  0.6 0.7 %copy-start.6 = (f32[1,20,25]{2,0,1:T(1,128)S(1)}, f32[1,20,25]{2,0,1:T(1,128)}, u32[]{:S(2)}) copy-start(f32[1,20,25]{2,0,1:T(1,128)} %param.13) | copy-start | bytes 6004
  1.3 0.7 %copy-start.3 = (s32[1,20]{1,0:T(1,128)S(1)}, s32[1,20]{1,0:T(1,128)}, u32[]{:S(2)}) copy-start(s32[1,20]{1,0:T(1,128)} %param.10) | copy-start | bytes 244
  1.3 0.7 %copy-start.4 = (s32[1,20]{1,0:T(1,128)S(1)}, s32[1,20]{1,0:T(1,128)}, u32[]{:S(2)}) copy-start(s32[1,20]{1,0:T(1,128)} %param.11) | copy-start | bytes 244
  1.3 0.7 %copy-start.5 = (s32[1,20]{1,0:T(1,128)S(1)}, s32[1,20]{1,0:T(1,128)}, u32[]{:S(2)}) copy-start(s32[1,20]{1,0:T(1,128)} %param.12) | copy-start | bytes 244
  2.0 1.2 %copy-start = (bf16[1,2,56,4096]{3,2,1,0:T(8,128)(2,1)S(1)}, bf16[1,2,56,4096]{3,2,1,0:T(8,128)(2,1)}, u32[]{:S(2)}) copy-start(bf16[1,2,56,4096]{3,2,1,0:T(8,128)(2,1)} %param.7) | copy-start | bytes 2752516
  3.2 1.0 %copy-start.1 = (bf16[1,20,25,256]{3,1,2,0:T(8,128)(2,1)S(1)}, bf16[1,20,25,256]{3,1,2,0:T(8,128)(2,1)}, u32[]{:S(2)}) copy-start(bf16[1,20,25,256]{3,1,2,0:T(8,128)(2,1)} %param.9) | copy-start | bytes 768004
  4.2 1.0 %copy-start.2 = (bf16[1,20,50,64]{3,2,1,0:T(8,128)(2,1)S(1)}, bf16[1,20,50,64]{3,2,1,0:T(8,128)(2,1)}, u32[]{:S(2)}) copy-start(bf16[1,20,50,64]{3,2,1,0:T(8,128)(2,1)} %param.8) | copy-start | bytes 384004

commit v4 on v3

--- a/solution.py
+++ b/solution.py
@@ -61,8 +61,9 @@
 
 def solve_kernel(
     count, group, frames,
-    row_off, col_off, dest, exposure, row_prof, col_prof, fibre_weight,
+    row_hbm, col_hbm, dest_hbm, exposure, row_prof, col_prof, fibre_weight,
     ext_out, coadd_out,
+    row_off, col_off, dest,
     pixels, rows_raw, cols_raw, weight_raw, low, high, ext, cols_wide, profile, cols,
     cut_weight, cut_value, inverse, direction, residual, spectra, norms, send, recv, contrib,
     arrived, mine, parts, sums,
@@ -94,7 +95,10 @@
     loads = [
         pltpu.make_async_copy(source, target, load_sem.at[i])
         for i, (source, target) in enumerate(
-            [(exposure, pixels), (row_prof, rows_raw), (col_prof, cols_raw), (fibre_weight, weight_raw)]
+            [
+                (exposure, pixels), (row_prof, rows_raw), (col_prof, cols_raw), (fibre_weight, weight_raw),
+                (row_hbm, row_off), (col_hbm, col_off), (dest_hbm, dest),
+            ]
         )
     ]
     for load in loads:
@@ -131,13 +135,27 @@
         cols[p] = jnp.concatenate([jnp.concatenate(taken, axis=1), gap], axis=0).astype(jnp.bfloat16)
 
     loads[0].wait()
+    for load in loads[3:]:
+        load.wait()
     for channel in range(2):
         for tile in range(tiles):
             at = slice(tile * LANES, (tile + 1) * LANES)
             ext[channel, tile, HALO:PR, :] = pixels[channel, :, at].astype(f32)
 
-    starts = [row_off[p] for p in range(count)]
-    columns = [col_off[p] for p in range(count)]
+    raw = jnp.concatenate([weight_raw[:, 0, :], jnp.zeros((count, LANES - FPB), f32)], axis=1)
+    weights = jnp.concatenate([raw, jnp.zeros((LANES - count, LANES), f32)], axis=0).T[0:32]
+
+    source = []
+    for d in range(group):
+        first = jnp.int32(count)
+        last = jnp.int32(count)
+        for p in range(count):
+            last = jnp.where(dest[0, p] == d, p, last)
+            first = jnp.where(dest[0, count - 1 - p] == d, count - 1 - p, first)
+        source.append((first, jnp.where(last == first, count, last)))
+
+    starts = [row_off[0, p] for p in range(count)]
+    columns = [col_off[0, p] for p in range(count)]
     firsts = [c // LANES for c in columns]
     shifts = [c - t * LANES for c, t in zip(columns, firsts)]
 
@@ -158,19 +176,6 @@
                 cut_value[p, j, first:first + size, :] = weight * value
 
     cut(HALO, PR - HALO)
-    loads[3].wait()
-    raw = jnp.concatenate([weight_raw[...], jnp.zeros((count, LANES - FPB), f32)], axis=1)
-    weights = jnp.concatenate([raw, jnp.zeros((LANES - count, LANES), f32)], axis=0).T[0:32]
-
-    source = []
-    for d in range(group):
-        first = jnp.int32(count)
-        last = jnp.int32(count)
-        for p in range(count):
-            last = jnp.where(dest[p] == d, p, last)
-            first = jnp.where(dest[count - 1 - p] == d, count - 1 - p, first)
-        source.append((first, jnp.where(last == first, count, last)))
-
     down.wait_recv()
     up.wait_recv()
     for channel in range(2):
@@ -313,7 +318,7 @@
 
 VMEM = pl.BlockSpec(memory_space=pltpu.VMEM)
 SMEM = pl.BlockSpec(memory_space=pltpu.SMEM)
-ANY = pl.BlockSpec(memory_space=pl.ANY)
+HBM = pl.BlockSpec(memory_space=pltpu.HBM)
 
 
 def local(exposure, row_prof, col_prof, row_off, col_off, dest, fibre_weight):
@@ -331,13 +336,16 @@
             jax.ShapeDtypeStruct((FPB, 2 * group, WPB), f32),
             jax.ShapeDtypeStruct((FPB, count, WPB), f32),
         ),
-        in_specs=[SMEM] * 3 + [ANY] * 4,
+        in_specs=[HBM] * 7,
         out_specs=(VMEM, VMEM),
         scratch_shapes=[
+            pltpu.SMEM((1, count), jnp.int32),
+            pltpu.SMEM((1, count), jnp.int32),
+            pltpu.SMEM((1, count), jnp.int32),
             pltpu.VMEM((channels, depth, width), bf16),
             pltpu.VMEM((count, WPB, PR), bf16),
             pltpu.VMEM((FPB, count, PC), bf16),
-            pltpu.VMEM((count, FPB), f32),
+            pltpu.VMEM((count, 1, FPB), f32),
             pltpu.VMEM((channels, HALO, width), bf16),
             pltpu.VMEM((channels, HALO, width), bf16),
             pltpu.VMEM((channels, tiles + 1, PR + HALO, LANES), f32),
@@ -358,7 +366,7 @@
             pltpu.VMEM((LANES, LANES), f32),
             pltpu.VMEM((chips, 32, LANES), f32),
             pltpu.VMEM((2, LANES, LANES), f32),
-            pltpu.SemaphoreType.DMA((4,)),
+            pltpu.SemaphoreType.DMA((7,)),
             pltpu.SemaphoreType.DMA((2,)),
             pltpu.SemaphoreType.DMA((2,)),
             pltpu.SemaphoreType.DMA((2,)),
@@ -375,8 +383,8 @@
             collective_id=0, has_side_effects=True, vmem_limit_bytes=48 << 20),
         name="solve",
     )(
-        row_off[0], col_off[0], dest[0], exposure[0], row_prof[0],
-        jnp.swapaxes(col_prof[0], 0, 1), fibre_weight[0],
+        *[pltpu.with_memory_space_constraint(a, pltpu.HBM) for a in (row_off, col_off, dest, exposure[0], row_prof[0],
+        jnp.swapaxes(col_prof[0], 0, 1), jnp.swapaxes(fibre_weight, 0, 1))],
     )
     return jnp.transpose(ext_out, (1, 2, 0))[None], jnp.transpose(coadd_out, (1, 2, 0))
 

time: 51.4 us -> 46.4 us (0.903)
  local copies, waits for them, and re-layouts: 5.95 us -> 1.47 us
    unnamed x17 -> x2, local copies, waits for them, and re-layouts: 5.95 us -> 1.47 us
where the time goes in v4:
time: 46.4 us
  Pallas kernels  44.2 us (95%)
  local copies, waits for them, and re-layouts  1.47 us (3%)
  between operations  0.64 us (1%)
    pallas_call x1, Pallas kernels, local(): pl.pallas_call(functools.partial(solve_kernel, count, group, frames), out...  44.2 us
    unnamed x2, local copies, waits for them, and re-layouts  1.47 us

profile of v4, /device:TPU:1, one launch (start us, length us, event | category | flops | bytes accessed | tf_op | source)
XLA Modules:
  0.0 46.4 jit_solution(1417596694068620316)
XLA Ops:
  0.6 44.2 %solve.1 = (f32[25,32,50]{2,1,0:T(8,128)S(1)}, f32[25,20,50]{2,1,0:T(8,128)S(1)}) custom-call(s32[1,20]{1,0:T(1,128)} %row_hbm.1, s32[1,20]{1,0:T(1,128)} %col_hbm.1, s32[1,20]{1,0:T(1,128)} %dest_hbm.1, bf16[2,56,4096]{2,1,0:T(8,128)(2,1)} %bitcast.12, bf16[20,50,64]{2,1,0:T(8,128)(2,1)} %bitcast.14, bf16[25,20,256]{2,1,0:T(8,128)(2,1)} %bitcast.13, ...), custom_call_target="tpu_custom_call" | custom-call | tf_op jit(solution)/shard_map/solve/pallas_call | solution.py:333
  44.9 0.8 %copy.11 = f32[1,32,50,25]{2,1,3,0:T(8,128)} copy(f32[1,32,50,25]{2,1,3,0:T(8,128)S(1)} %bitcast.10) | data formatting | bytes 320000
  45.6 0.7 %copy.12 = f32[20,50,25]{1,0,2:T(8,128)} copy(f32[20,50,25]{1,0,2:T(8,128)S(1)} %bitcast.11) | data formatting | bytes 200000

commit v5 on v4

--- a/solution.py
+++ b/solution.py
@@ -14,6 +14,7 @@
 LANES = 128
 WPB = 50
 FPB = 25
+SPREAD = 2
 MESH = pl.DeviceIdType.MESH
 NT = (((1,), (1,)), ((), ()))
 
@@ -27,19 +28,26 @@
     return jnp.where(first, value, value - head).astype(jnp.bfloat16)
 
 
-def project(weighted, cols, profile, half):
+def fold(weighted, cols):
     head = [g.astype(jnp.bfloat16) for g in weighted]
     tail = [(g - h.astype(jnp.float32)).astype(jnp.bfloat16) for g, h in zip(weighted, head)]
-    both = [jnp.concatenate([h, t], axis=0) for h, t in zip(head, tail)]
-    folded = [
-        lax.dot_general(c, g, NT, preferred_element_type=jnp.float32) for c, g in zip(cols, both)
-    ]
+    return [
+        lax.dot_general(c, jnp.concatenate([h, t], axis=0), NT, preferred_element_type=jnp.float32)
+        for c, h, t in zip(cols, head, tail)
+    ]
+
+
+def unfold(folded, profile, half):
     folded = [f + pltpu.roll(f, LANES // 2, 1) for f in folded]
     pieces = [second_piece(f, half) for f in folded]
     return [
         jnp.dot(f, jnp.concatenate([r, r], axis=0), preferred_element_type=jnp.float32)
         for f, r in zip(pieces, profile)
     ]
+
+
+def project(weighted, cols, profile, half):
+    return unfold(fold(weighted, cols), profile, half)
 
 
 def image_of(direction, cols, profile, half, quarter):
@@ -66,8 +74,9 @@
     row_off, col_off, dest,
     pixels, rows_raw, cols_raw, weight_raw, low, high, ext, cols_wide, profile, cols,
     cut_weight, cut_value, inverse, direction, residual, spectra, norms, send, recv, contrib,
-    arrived, mine, parts, sums,
-    load_sem, halo_out, halo_in, swap_sem, out_sem, in_sem, part_out, part_in, sum_out, sum_in, fwd_out, fwd_in,
+    arrived, gathered, sums,
+    load_sem, halo_out, halo_in, swap_out, swap_in, out_sem, in_sem, direct_out, direct_in, relay_out, relay_in,
+    fwd_out, fwd_in,
 ):
     f32 = jnp.float32
     section = lax.axis_index("section")
@@ -88,7 +97,7 @@
 
     barrier = pltpu.get_barrier_semaphore()
     inner = [{"patch": lax.rem(me + k, group)} for k in range(1, group)]
-    peers = [{"frame": lax.rem(frame + 2 * k, frames)} for k in range(1, chips)]
+    peers = [{"frame": lax.rem(frame + step, frames)} for step in (2, frames - 2)]
     partners = [at_band(above), at_band(below)] + [{"frame": partner}] + peers + inner
     for device in partners:
         pl.semaphore_signal(barrier, inc=1, device_id=device, device_id_type=MESH)
@@ -188,48 +197,76 @@
     cut(PR, HALO)
 
     every = list(range(count))
-    c = [cols[p] for p in every]
-    r = [profile[p] for p in every]
-    weighted = []
-    for p in every:
+    def begin(p):
         inverse[p] = jnp.concatenate([cut_weight[p, j, pl.ds(starts[p], PR), :] for j in range(2)], axis=1)
-        weighted.append(
-            jnp.concatenate([cut_value[p, j, pl.ds(starts[p], PR), :] for j in range(2)], axis=1))
-    for p, value in zip(every, project(weighted, c, r, half)):
-        direction[p] = value
-        residual[p] = value
-        spectra[p] = jnp.zeros_like(value)
-        norms[p] = jnp.broadcast_to(total(value * value), (8, LANES))
+        value = jnp.concatenate([cut_value[p, j, pl.ds(starts[p], PR), :] for j in range(2)], axis=1)
+        folded = fold([value], [cols[p]])
+        yield
+        rhs = unfold(folded, [profile[p]], half)[0]
+        yield
+        direction[p] = rhs
+        residual[p] = rhs
+        spectra[p] = jnp.zeros_like(rhs)
+        norms[p] = jnp.broadcast_to(total(rhs * rhs), (8, LANES))
+        yield
+
+    def model(p):
+        pieces = second_piece(direction[p], half)
+        across = lax.dot_general(
+            profile[p], jnp.concatenate([pieces, pieces], axis=0), NT, preferred_element_type=f32)
+        yield
+        pieces = second_piece(across, quarter)
+        modeled = jnp.dot(pieces, jnp.concatenate([cols[p], cols[p]], axis=0), preferred_element_type=f32)
+        yield
+        return modeled
+
+    def iterate(p):
+        modeled = yield from model(p)
+        folded = fold([inverse[p] * modeled], [cols[p]])
+        yield
+        imaged = unfold(folded, [profile[p]], half)[0]
+        yield
+        curvature = total(direction[p] * imaged)
+        yield
+        now = norms[p][0:1, 0:1]
+        size = now / jnp.where(curvature > 0.0, curvature, 1.0)
+        left = residual[p] - size * imaged
+        residual[p] = left
+        spectra[p] += size * direction[p]
+        later = total(left * left)
+        yield
+        norms[p] = jnp.broadcast_to(later, (8, LANES))
+        direction[p] = residual[p] + later / jnp.where(now > 0.0, now, 1.0) * direction[p]
+        yield
+
+    def conclude(p):
+        modeled = yield from model(p)
+        curvature = 2.0 * total(jnp.sum(inverse[p] * modeled * modeled, axis=0, keepdims=True))
+        yield
+        spectra[p] += norms[p][0:1, 0:1] / jnp.where(curvature > 0.0, curvature, 1.0) * direction[p]
+        yield
+
+    def emit(chain, spread):
+        pending = {p: chain(p) for p in every}
+        key = {p: p * spread for p in every}
+        while pending:
+            p = min(pending, key=lambda q: (key[q], q))
+            key[p] += count
+            try:
+                next(pending[p])
+            except StopIteration:
+                del pending[p]
+
+    def whole_chain(p):
+        yield from begin(p)
+        for _ in range(ITERS - 1):
+            yield from iterate(p)
+        yield from conclude(p)
+
+    emit(whole_chain, SPREAD)
     spectra[count] = jnp.zeros((32, LANES), f32)
 
-    def sweep(index, carry):
-        c = [cols[p] for p in every]
-        r = [profile[p] for p in every]
-        along = [direction[p] for p in every]
-        modeled = image_of(along, c, r, half, quarter)
-        imaged = project([inverse[p] * m for p, m in zip(every, modeled)], c, r, half)
-        curvature = [total(d * q) for d, q in zip(along, imaged)]
-        now = [norms[p][0:1, 0:1] for p in every]
-        size = [n / jnp.where(k > 0.0, k, 1.0) for n, k in zip(now, curvature)]
-        left = [residual[p] - a * q for p, a, q in zip(every, size, imaged)]
-        later = [total(e * e) for e in left]
-        ratio = [n / jnp.where(b > 0.0, b, 1.0) for n, b in zip(later, now)]
-        for p, a, d, e, n, k in zip(every, size, along, left, later, ratio):
-            spectra[p] += a * d
-            residual[p] = e
-            norms[p] = jnp.broadcast_to(n, (8, LANES))
-            direction[p] = e + k * d
-        return carry
-
-    lax.fori_loop(0, ITERS - 1, sweep, 0)
-    along = [direction[p] for p in every]
-    modeled = image_of(along, [cols[p] for p in every], [profile[p] for p in every], half, quarter)
-    curvature = [
-        2.0 * total(jnp.sum(inverse[p] * m * m, axis=0, keepdims=True)) for p, m in zip(every, modeled)
-    ]
-    for p, d, k in zip(every, along, curvature):
-        spectra[p] += norms[p][0:1, 0:1] / jnp.where(k > 0.0, k, 1.0) * d
-
+    blocks = [slice(0, LANES // 2), slice(LANES // 2, LANES)]
     pairs = count // 2
     per_half = pairs // 2
     marked = lane_index((32, LANES)) % (LANES // 2) == WPB
@@ -243,56 +280,67 @@
         contrib[j // per_half, start:start + FPB, :] = value[0:FPB]
     for h in range(2):
         contrib[h, per_half * FPB:, :] = jnp.zeros((LANES - per_half * FPB, LANES), f32)
-    swap = pltpu.make_async_remote_copy(
-        contrib.at[1 - core], arrived, swap_sem.at[0], swap_sem.at[1],
-        device_id={"frame": partner}, device_id_type=MESH)
-    swap.start()
+    swaps = [
+        pltpu.make_async_remote_copy(
+            contrib.at[1 - core, part], arrived.at[part], swap_out.at[i], swap_in.at[i],
+            device_id={"frame": partner}, device_id_type=MESH)
+        for i, part in enumerate(blocks)
+    ]
+    for copy in swaps:
+        copy.start()
     for d in range(group):
         send[d] = jnp.where(half, spectra[source[d][0]], spectra[source[d][1]])[0:FPB]
-    spread = []
-    for k in range(1, group):
-        to = lax.rem(me + k, group)
-        spread.append(pltpu.make_async_remote_copy(
+    side = group // 2
+    near = [lax.div(me, side) * side + lax.rem(me + k, side) for k in range(1, side)]
+    far = [(1 - lax.div(me, side)) * side + lax.rem(me + k, side) for k in range(side)]
+    spread = [
+        pltpu.make_async_remote_copy(
             send.at[to], recv.at[me], out_sem.at[k], in_sem.at[k],
-            device_id={"patch": to}, device_id_type=MESH))
-        spread[-1].start()
-
-    def chunk(index):
-        return pl.ds(pl.multiple_of(index * 32, 32), 32)
-
-    swap.wait()
-    mine[...] = contrib[core] + arrived[...]
-    scatter = []
-    for k in range(1, chips):
-        to = lax.rem(chip + k, chips)
-        scatter.append(pltpu.make_async_remote_copy(
-            mine.at[chunk(to)], parts.at[chip], part_out.at[k], part_in.at[k],
-            device_id={"frame": 2 * to + core}, device_id_type=MESH))
-        scatter[-1].start()
-    parts[chip] = mine[chunk(chip), :]
+            device_id={"patch": to}, device_id_type=MESH)
+        for k, to in enumerate(near + far)
+    ]
+    for copy in spread[:side - 1]:
+        copy.start()
+
+    after, before = lax.rem(chip + 1, chips), lax.rem(chip + chips - 1, chips)
+
+    def pass_on(owner, part, forward, out_sem, in_sem):
+        return pltpu.make_async_remote_copy(
+            gathered.at[owner, part], gathered.at[owner, part], out_sem, in_sem,
+            device_id={"frame": 2 * (after if forward else before) + core}, device_id_type=MESH)
+
+    for copy, part in zip(swaps, blocks):
+        copy.wait_recv()
+        gathered[chip, part, :] = contrib[core, part, :] + arrived[part, :]
+    ahead = [pass_on(chip, part, True, direct_out.at[i], direct_in.at[i]) for i, part in enumerate(blocks)]
+    back = [
+        pass_on(chip, part, False, direct_out.at[2 + i], direct_in.at[2 + i])
+        for i, part in enumerate(blocks)
+    ]
+    for copy in (ahead[0], back[1], ahead[1], back[0]):
+        copy.start()
+    for copy in spread[side - 1:]:
+        copy.start()
     recv[me] = send[me]
-    for copy in scatter:
-        copy.wait_recv()
-    whole = parts[0]
-    for k in range(1, chips):
-        whole = whole + parts[k]
-    sums[core, chunk(chip), :] = whole
-    gather = []
-    for k in range(1, chips):
-        to = lax.rem(chip + k, chips)
-        gather.append(pltpu.make_async_remote_copy(
-            sums.at[core, chunk(chip)], sums.at[core, chunk(chip)], sum_out.at[k], sum_in.at[k],
-            device_id={"frame": 2 * to + core}, device_id_type=MESH))
-        gather[-1].start()
+    ahead[0].wait_recv()
+    relays = [pass_on(before, blocks[0], True, relay_out.at[0], relay_in.at[0])]
+    relays[0].start()
+    back[1].wait_recv()
+    relays.append(pass_on(after, blocks[1], False, relay_out.at[1], relay_in.at[1]))
+    relays[1].start()
+    ahead[1].wait_recv()
+    back[0].wait_recv()
     forward = []
-    for k in range(chips):
-        from_chip = lax.rem(chip + chips - k, chips)
-        if k:
-            gather[k - 1].wait_recv()
+    for i, part in enumerate(blocks):
+        relays[i].wait_recv()
+        whole = gathered[0, part, :]
+        for k in range(1, chips):
+            whole = whole + gathered[k, part, :]
+        sums[core, part, :] = whole
         forward.append(pltpu.make_async_remote_copy(
-            sums.at[core, chunk(from_chip)], sums.at[core, chunk(from_chip)], fwd_out.at[k], fwd_in.at[k],
+            sums.at[core, part], sums.at[core, part], fwd_out.at[i], fwd_in.at[i],
             device_id={"frame": partner}, device_id_type=MESH))
-        forward[-1].start()
+        forward[i].start()
 
     for copy in spread:
         copy.wait_recv()
@@ -311,8 +359,7 @@
                 coadd_out[k, start:start + per_half, :] = here[:, 0:WPB] / here[:, WPB:WPB + 1]
     down.wait_send()
     up.wait_send()
-    swap_done = scatter + gather + forward + spread
-    for copy in swap_done:
+    for copy in swaps + ahead + back + relays + forward + spread:
         copy.wait_send()
 
 
@@ -363,21 +410,21 @@
             pltpu.VMEM((group, FPB, LANES), f32),
             pltpu.VMEM((2, LANES, LANES), f32),
             pltpu.VMEM((LANES, LANES), f32),
-            pltpu.VMEM((LANES, LANES), f32),
-            pltpu.VMEM((chips, 32, LANES), f32),
+            pltpu.VMEM((chips, LANES, LANES), f32),
             pltpu.VMEM((2, LANES, LANES), f32),
             pltpu.SemaphoreType.DMA((7,)),
             pltpu.SemaphoreType.DMA((2,)),
             pltpu.SemaphoreType.DMA((2,)),
             pltpu.SemaphoreType.DMA((2,)),
+            pltpu.SemaphoreType.DMA((2,)),
             pltpu.SemaphoreType.DMA((group,)),
             pltpu.SemaphoreType.DMA((group,)),
-            pltpu.SemaphoreType.DMA((chips,)),
-            pltpu.SemaphoreType.DMA((chips,)),
-            pltpu.SemaphoreType.DMA((chips,)),
-            pltpu.SemaphoreType.DMA((chips,)),
-            pltpu.SemaphoreType.DMA((chips,)),
-            pltpu.SemaphoreType.DMA((chips,)),
+            pltpu.SemaphoreType.DMA((4,)),
+            pltpu.SemaphoreType.DMA((4,)),
+            pltpu.SemaphoreType.DMA((2,)),
+            pltpu.SemaphoreType.DMA((2,)),
+            pltpu.SemaphoreType.DMA((2,)),
+            pltpu.SemaphoreType.DMA((2,)),
         ],
         compiler_params=pltpu.CompilerParams(
             collective_id=0, has_side_effects=True, vmem_limit_bytes=48 << 20),

time: 46.4 us -> 44.1 us (0.950)
  Pallas kernels: 44.2 us -> 41.9 us
    pallas_call x1, Pallas kernels: 44.2 us -> 41.9 us  [local(): pl.pallas_call(functools.partial(solve_kernel, count, group, frames), out...]
where the time goes in v5:
time: 44.1 us; the launch traced here: 44 us
  Pallas kernels  41.9 us (95%)
  local copies, waits for them, and re-layouts  1.47 us (3%)
  between operations  0.64 us (1%)
    pallas_call x1, Pallas kernels, local(): pl.pallas_call(functools.partial(solve_kernel, count, group, frames), out...  41.9 us
    unnamed x2, local copies, waits for them, and re-layouts  1.47 us

profile of v5, /device:TPU:1, one launch (start us, length us, event | category | flops | bytes accessed | tf_op | source)
XLA Modules:
  0.0 44.0 jit_solution(1565986024878014886)
XLA Ops:
  0.6 41.9 %solve.1 = (f32[25,32,50]{2,1,0:T(8,128)S(1)}, f32[25,20,50]{2,1,0:T(8,128)S(1)}) custom-call(s32[1,20]{1,0:T(1,128)} %row_hbm.1, s32[1,20]{1,0:T(1,128)} %col_hbm.1, s32[1,20]{1,0:T(1,128)} %dest_hbm.1, bf16[2,56,4096]{2,1,0:T(8,128)(2,1)} %bitcast.12, bf16[20,50,64]{2,1,0:T(8,128)(2,1)} %bitcast.14, bf16[25,20,256]{2,1,0:T(8,128)(2,1)} %bitcast.13, ...), custom_call_target="tpu_custom_call" | custom-call | tf_op jit(solution)/shard_map/solve/pallas_call | solution.py:380
  42.6 0.8 %copy.11 = f32[1,32,50,25]{2,1,3,0:T(8,128)} copy(f32[1,32,50,25]{2,1,3,0:T(8,128)S(1)} %bitcast.10) | data formatting | bytes 320000
  43.3 0.7 %copy.12 = f32[20,50,25]{1,0,2:T(8,128)} copy(f32[20,50,25]{1,0,2:T(8,128)S(1)} %bitcast.11) | data formatting | bytes 200000

commit v6 on v5

--- a/solution.py
+++ b/solution.py
@@ -246,9 +246,9 @@
         spectra[p] += norms[p][0:1, 0:1] / jnp.where(curvature > 0.0, curvature, 1.0) * direction[p]
         yield
 
-    def emit(chain, spread):
-        pending = {p: chain(p) for p in every}
-        key = {p: p * spread for p in every}
+    def emit(chain, spread, order, hooks):
+        pending = {p: chain(p) for p in order}
+        key = {p: i * spread for i, p in enumerate(order)}
         while pending:
             p = min(pending, key=lambda q: (key[q], q))
             key[p] += count
@@ -256,6 +256,8 @@
                 next(pending[p])
             except StopIteration:
                 del pending[p]
+            while hooks and not set(hooks[0][0]) & set(pending):
+                hooks.pop(0)[1]()
 
     def whole_chain(p):
         yield from begin(p)
@@ -263,31 +265,40 @@
             yield from iterate(p)
         yield from conclude(p)
 
-    emit(whole_chain, SPREAD)
-    spectra[count] = jnp.zeros((32, LANES), f32)
-
-    blocks = [slice(0, LANES // 2), slice(LANES // 2, LANES)]
     pairs = count // 2
     per_half = pairs // 2
     marked = lane_index((32, LANES)) % (LANES // 2) == WPB
-    for j in range(pairs):
-        scale = jnp.where(
-            half,
-            jnp.broadcast_to(weights[:, j:j + 1], (32, LANES)),
-            jnp.broadcast_to(weights[:, pairs + j:pairs + j + 1], (32, LANES)))
-        value = scale * jnp.where(marked, 1.0, jnp.where(half, spectra[j], spectra[pairs + j]))
-        start = (j % per_half) * FPB
-        contrib[j // per_half, start:start + FPB, :] = value[0:FPB]
-    for h in range(2):
-        contrib[h, per_half * FPB:, :] = jnp.zeros((LANES - per_half * FPB, LANES), f32)
+    blocks = [slice(0, LANES // 2), slice(LANES // 2, LANES)]
+    cuts = [part.stop // FPB + 1 if part.stop < LANES else per_half for part in blocks]
     swaps = [
         pltpu.make_async_remote_copy(
             contrib.at[1 - core, part], arrived.at[part], swap_out.at[i], swap_in.at[i],
             device_id={"frame": partner}, device_id_type=MESH)
         for i, part in enumerate(blocks)
     ]
-    for copy in swaps:
-        copy.start()
+
+    def contribute(first, last, swap):
+        for j in range(pairs):
+            if not first <= j % per_half < last:
+                continue
+            scale = jnp.where(
+                half,
+                jnp.broadcast_to(weights[:, j:j + 1], (32, LANES)),
+                jnp.broadcast_to(weights[:, pairs + j:pairs + j + 1], (32, LANES)))
+            value = scale * jnp.where(marked, 1.0, jnp.where(half, spectra[j], spectra[pairs + j]))
+            start = (j % per_half) * FPB
+            contrib[j // per_half, start:start + FPB, :] = value[0:FPB]
+        swap.start()
+
+    for h in range(2):
+        contrib[h, per_half * FPB:, :] = jnp.ones((LANES - per_half * FPB, LANES), f32)
+    groups = [[p for p in every if p % per_half < cuts[0]], [p for p in every if p % per_half >= cuts[0]]]
+    emit(whole_chain, SPREAD, groups[0] + groups[1], [
+        (groups[0], lambda: contribute(0, cuts[0], swaps[0])),
+        (groups[1], lambda: contribute(cuts[0], per_half, swaps[1])),
+    ])
+    spectra[count] = jnp.zeros((32, LANES), f32)
+
     for d in range(group):
         send[d] = jnp.where(half, spectra[source[d][0]], spectra[source[d][1]])[0:FPB]
     side = group // 2
@@ -336,7 +347,11 @@
         whole = gathered[0, part, :]
         for k in range(1, chips):
             whole = whole + gathered[k, part, :]
-        sums[core, part, :] = whole
+        mass = jnp.where(
+            lane_index(whole.shape) < LANES // 2,
+            jnp.broadcast_to(whole[:, WPB:WPB + 1], whole.shape),
+            jnp.broadcast_to(whole[:, LANES // 2 + WPB:LANES // 2 + WPB + 1], whole.shape))
+        sums[core, part, :] = whole / mass
         forward.append(pltpu.make_async_remote_copy(
             sums.at[core, part], sums.at[core, part], fwd_out.at[i], fwd_in.at[i],
             device_id={"frame": partner}, device_id_type=MESH))
@@ -356,11 +371,22 @@
             for s in range(2):
                 here = rows if s == 0 else pltpu.roll(rows, LANES // 2, 1)
                 start = s * pairs + h * per_half
-                coadd_out[k, start:start + per_half, :] = here[:, 0:WPB] / here[:, WPB:WPB + 1]
+                coadd_out[k, start:start + per_half, :] = here[:, 0:WPB]
     down.wait_send()
     up.wait_send()
     for copy in swaps + ahead + back + relays + forward + spread:
         copy.wait_send()
+
+
+def settle_kernel(ext_in, coadd_in, ext_out, coadd_out, sem):
+    copies = [
+        pltpu.make_async_copy(ext_in, ext_out, sem.at[0]),
+        pltpu.make_async_copy(coadd_in, coadd_out, sem.at[1]),
+    ]
+    for copy in copies:
+        copy.start()
+    for copy in copies:
+        copy.wait()
 
 
 VMEM = pl.BlockSpec(memory_space=pltpu.VMEM)
@@ -433,6 +459,15 @@
         *[pltpu.with_memory_space_constraint(a, pltpu.HBM) for a in (row_off, col_off, dest, exposure[0], row_prof[0],
         jnp.swapaxes(col_prof[0], 0, 1), jnp.swapaxes(fibre_weight, 0, 1))],
     )
+    ext_out, coadd_out = pl.pallas_call(
+        settle_kernel,
+        out_shape=tuple(jax.ShapeDtypeStruct(a.shape, f32) for a in (ext_out, coadd_out)),
+        in_specs=[VMEM] * 2,
+        out_specs=(HBM, HBM),
+        scratch_shapes=[pltpu.SemaphoreType.DMA((2,))],
+        compiler_params=pltpu.CompilerParams(vmem_limit_bytes=8 << 20),
+        name="settle",
+    )(ext_out, coadd_out)
     return jnp.transpose(ext_out, (1, 2, 0))[None], jnp.transpose(coadd_out, (1, 2, 0))
 
 

time: 44.1 us -> 42.6 us (0.966)
  local copies, waits for them, and re-layouts: 1.47 us -> 0 us
    unnamed x2 -> x0, local copies, waits for them, and re-layouts: 1.47 us -> none
    pallas_call x1, Pallas kernels: 41.9 us -> 41 us  [local(): pl.pallas_call(functools.partial(solve_kernel, count, group, frames), out...]
    pallas_call x0 -> x1, Pallas kernels: none -> 0.85 us  [local(): pl.pallas_call(settle_kernel, out_shape=tuple((jax.ShapeDtypeStruct(a.sha...]
where the time goes in v6:
time: 42.6 us; the launch traced here: 42.5 us
  Pallas kernels  41.8 us (98%)
  between operations  0.64 us (2%)
    pallas_call x1, Pallas kernels, local(): pl.pallas_call(functools.partial(solve_kernel, count, group, frames), out...  41 us

profile of v6, /device:TPU:1, one launch (start us, length us, event | category | flops | bytes accessed | tf_op | source)
XLA Modules:
  0.0 42.5 jit_solution(7908831768263217112)
XLA Ops:
  0.6 41.0 %solve.1 = (f32[25,32,50]{2,1,0:T(8,128)S(1)}, f32[25,20,50]{2,1,0:T(8,128)S(1)}) custom-call(s32[1,20]{1,0:T(1,128)} %row_hbm.1, s32[1,20]{1,0:T(1,128)} %col_hbm.1, s32[1,20]{1,0:T(1,128)} %dest_hbm.1, bf16[2,56,4096]{2,1,0:T(8,128)(2,1)} %bitcast.10, bf16[20,50,64]{2,1,0:T(8,128)(2,1)} %bitcast.12, bf16[25,20,256]{2,1,0:T(8,128)(2,1)} %bitcast.11, ...), custom_call_target="tpu_custom_call" | custom-call | tf_op jit(solution)/shard_map/solve/pallas_call | solution.py:406
  41.6 0.9 %settle.1 = (f32[25,32,50]{2,1,0:T(8,128)}, f32[25,20,50]{2,1,0:T(8,128)}) custom-call(f32[25,32,50]{2,1,0:T(8,128)S(1)} %get-tuple-element.6.ext_in, f32[25,20,50]{2,1,0:T(8,128)S(1)} %get-tuple-element.7.coadd_in), custom_call_target="tpu_custom_call" | custom-call | tf_op jit(solution)/shard_map/settle/pallas_call | solution.py:462

commit v7 on v6

--- a/solution.py
+++ b/solution.py
@@ -308,9 +308,9 @@
         pltpu.make_async_remote_copy(
             send.at[to], recv.at[me], out_sem.at[k], in_sem.at[k],
             device_id={"patch": to}, device_id_type=MESH)
-        for k, to in enumerate(near + far)
-    ]
-    for copy in spread[:side - 1]:
+        for k, to in enumerate(far + near)
+    ]
+    for copy in spread[:side]:
         copy.start()
 
     after, before = lax.rem(chip + 1, chips), lax.rem(chip + chips - 1, chips)
@@ -330,7 +330,7 @@
     ]
     for copy in (ahead[0], back[1], ahead[1], back[0]):
         copy.start()
-    for copy in spread[side - 1:]:
+    for copy in spread[side:]:
         copy.start()
     recv[me] = send[me]
     ahead[0].wait_recv()

time: 42.6 us -> 41.2 us (0.967)
  Pallas kernels: 41.8 us -> 40.4 us
    pallas_call x1, Pallas kernels: 41 us -> 39.6 us  [local(): pl.pallas_call(functools.partial(solve_kernel, count, group, frames), out...]
where the time goes in v7:
time: 41.2 us; the launch traced here: 41.1 us
  Pallas kernels  40.4 us (98%)
  between operations  0.64 us (2%)
    pallas_call x1, Pallas kernels, local(): pl.pallas_call(functools.partial(solve_kernel, count, group, frames), out...  39.6 us
    pallas_call x1, Pallas kernels, local(): pl.pallas_call(settle_kernel, out_shape=tuple((jax.ShapeDtypeStruct(a.sha...  0.85 us

profile of v7, /device:TPU:1, one launch (start us, length us, event | category | flops | bytes accessed | tf_op | source)
XLA Modules:
  0.0 41.1 jit_solution(7967542312250609167)
XLA Ops:
  0.6 39.6 %solve.1 = (f32[25,32,50]{2,1,0:T(8,128)S(1)}, f32[25,20,50]{2,1,0:T(8,128)S(1)}) custom-call(s32[1,20]{1,0:T(1,128)} %row_hbm.1, s32[1,20]{1,0:T(1,128)} %col_hbm.1, s32[1,20]{1,0:T(1,128)} %dest_hbm.1, bf16[2,56,4096]{2,1,0:T(8,128)(2,1)} %bitcast.10, bf16[20,50,64]{2,1,0:T(8,128)(2,1)} %bitcast.12, bf16[25,20,256]{2,1,0:T(8,128)(2,1)} %bitcast.11, ...), custom_call_target="tpu_custom_call" | custom-call | tf_op jit(solution)/shard_map/solve/pallas_call | solution.py:406
  40.2 0.9 %settle.1 = (f32[25,32,50]{2,1,0:T(8,128)}, f32[25,20,50]{2,1,0:T(8,128)}) custom-call(f32[25,32,50]{2,1,0:T(8,128)S(1)} %get-tuple-element.6.ext_in, f32[25,20,50]{2,1,0:T(8,128)S(1)} %get-tuple-element.7.coadd_in), custom_call_target="tpu_custom_call" | custom-call | tf_op jit(solution)/shard_map/settle/pallas_call | solution.py:462

commit v8 on v7

--- a/solution.py
+++ b/solution.py
@@ -310,7 +310,7 @@
             device_id={"patch": to}, device_id_type=MESH)
         for k, to in enumerate(far + near)
     ]
-    for copy in spread[:side]:
+    for copy in spread:
         copy.start()
 
     after, before = lax.rem(chip + 1, chips), lax.rem(chip + chips - 1, chips)
@@ -329,8 +329,6 @@
         for i, part in enumerate(blocks)
     ]
     for copy in (ahead[0], back[1], ahead[1], back[0]):
-        copy.start()
-    for copy in spread[side:]:
         copy.start()
     recv[me] = send[me]
     ahead[0].wait_recv()

time: 41.2 us -> 41.4 us (level)
  no operation moved by 1% of the time
where the time goes in v8:
time: 41.4 us; the launch traced here: 41.3 us
  Pallas kernels  40.6 us (98%)
  between operations  0.64 us (2%)
    pallas_call x1, Pallas kernels, local(): pl.pallas_call(functools.partial(solve_kernel, count, group, frames), out...  39.8 us
    pallas_call x1, Pallas kernels, local(): pl.pallas_call(settle_kernel, out_shape=tuple((jax.ShapeDtypeStruct(a.sha...  0.85 us

profile of v8, /device:TPU:1, one launch (start us, length us, event | category | flops | bytes accessed | tf_op | source)
XLA Modules:
  0.0 41.3 jit_solution(1618703451331642268)
XLA Ops:
  0.6 39.8 %solve.1 = (f32[25,32,50]{2,1,0:T(8,128)S(1)}, f32[25,20,50]{2,1,0:T(8,128)S(1)}) custom-call(s32[1,20]{1,0:T(1,128)} %row_hbm.1, s32[1,20]{1,0:T(1,128)} %col_hbm.1, s32[1,20]{1,0:T(1,128)} %dest_hbm.1, bf16[2,56,4096]{2,1,0:T(8,128)(2,1)} %bitcast.10, bf16[20,50,64]{2,1,0:T(8,128)(2,1)} %bitcast.12, bf16[25,20,256]{2,1,0:T(8,128)(2,1)} %bitcast.11, ...), custom_call_target="tpu_custom_call" | custom-call | tf_op jit(solution)/shard_map/solve/pallas_call | solution.py:404
  40.4 0.9 %settle.1 = (f32[25,32,50]{2,1,0:T(8,128)}, f32[25,20,50]{2,1,0:T(8,128)}) custom-call(f32[25,32,50]{2,1,0:T(8,128)S(1)} %get-tuple-element.6.ext_in, f32[25,20,50]{2,1,0:T(8,128)S(1)} %get-tuple-element.7.coadd_in), custom_call_target="tpu_custom_call" | custom-call | tf_op jit(solution)/shard_map/settle/pallas_call | solution.py:460
